TPU v7x, 32 devices: a whole 2x2x4 slice. The times are simulated.
32 devices in a mesh: ea: 16 (over z, y, x), ta: 2 (over core).
Axes of the slice: x: 2, y: 2, z: 4, core: 2. Of those that a mesh axis runs over, the one named last changes fastest.
Arguments:
- sample_inphase: float32 [128, 256, 256], P('ea'), may hold values from 0.2 to 1.2
- sample_quadrature: float32 [128, 256, 256], P('ea'), may hold values from -3 to 3
- beam_inphase: float32 [128, 3, 32, 32], P('ea'), may hold values from -3 to 3
- beam_quadrature: float32 [128, 3, 32, 32], P('ea'), may hold values from -3 to 3
- recorded_diffraction: float32 [128, 2, 16, 32, 32], P('ea', 'ta'), may hold values from 0.05 to 4
- window_corners: int32 [128, 2, 16, 2], P('ea', 'ta'), may hold values from 0 to 224
- filled_tallies: int32 [128, 2], P('ea', 'ta'), may hold values from 1 to 16, 24 in all within a row
- absorption_templates: float32 [16, 128], replicated, may hold values from -6 to 6
Outputs:
- fitted: float32 [2, 128, 16, 2, 2048], P(None, 'ea', None, 'ta')
- coefficients: float32 [2, 16, 65536], P(None, None, ('ea', 'ta'))
Inputs may be any that keep to these rules, and one draw needn't show every extreme that they name: `filled_tallies`: in each energy the two tiles' counts sum to 24 and the larger is at most 16. `window_corners`: offsets of slots at or past their tile's count are not used.
All inputs are finite; a program needn't handle non-finite values. No bound on the sum of `filled_tallies` on one device may be relied on, other than what follows from the above.
Results may differ from a plain program's by a relative error of at most 0.0003.
Values sent between devices are 32-bit elements; how exact they have to be, the bound alone decides.
No kernel may reach another device: no remote copies, remote signals or barrier semaphores. Data moves between devices by JAX's collectives and lax.ppermute only.
A program may use at most 64 MiB of HBM per device.

v0:
```python
import jax
import jax.numpy as jnp
from jax import lax
from jax.sharding import PartitionSpec as P

HIGHEST_PRECISION = lax.Precision.HIGHEST
FLOOR_POWER = 0.5
REGULARIZER = 1.0


def dft_tables(length):
    counter = jnp.arange(length, dtype=jnp.int32)
    product = counter[:, None] * counter[None, :] % length
    angles = 2.0 * jnp.pi / length * product.astype(jnp.float32)
    norming = 1.0 / jnp.sqrt(jnp.float32(length))
    return (jnp.cos(angles) * norming, -jnp.sin(angles) * norming)


def two_sided(field_re, field_im, table_re, table_im):
    left_re = jnp.einsum(
        "jk,...kl->...jl", table_re, field_re, precision=HIGHEST_PRECISION
    ) - jnp.einsum("jk,...kl->...jl", table_im, field_im, precision=HIGHEST_PRECISION)
    left_im = jnp.einsum(
        "jk,...kl->...jl", table_re, field_im, precision=HIGHEST_PRECISION
    ) + jnp.einsum("jk,...kl->...jl", table_im, field_re, precision=HIGHEST_PRECISION)
    right_re = jnp.einsum(
        "...jk,kl->...jl", left_re, table_re, precision=HIGHEST_PRECISION
    ) - jnp.einsum("...jk,kl->...jl", left_im, table_im, precision=HIGHEST_PRECISION)
    right_im = jnp.einsum(
        "...jk,kl->...jl", left_re, table_im, precision=HIGHEST_PRECISION
    ) + jnp.einsum("...jk,kl->...jl", left_im, table_re, precision=HIGHEST_PRECISION)
    return (right_re, right_im)


def slot_terms(
    sample_inphase,
    sample_quadrature,
    beam_inphase,
    beam_quadrature,
    intensity,
    corners,
    weight,
    table_re,
    table_im,
):
    width = beam_inphase.shape[-1]

    def extract(source, corner):
        return lax.dynamic_slice(source, (corner[0], corner[1]), (width, width))

    patch_re = jax.vmap(extract, (None, 0))(sample_inphase, corners)
    patch_im = jax.vmap(extract, (None, 0))(sample_quadrature, corners)
    exit_re = beam_inphase[None] * patch_re[:, None] - beam_quadrature[None] * patch_im[:, None]
    exit_im = beam_inphase[None] * patch_im[:, None] + beam_quadrature[None] * patch_re[:, None]
    far_re, far_im = two_sided(exit_re, exit_im, table_re, table_im)
    power = jnp.sum(far_re * far_re + far_im * far_im, axis=1)
    factor = (1.0 - jnp.sqrt(intensity) / jnp.sqrt(jnp.maximum(power, FLOOR_POWER))) * weight[
        :, None, None
    ]
    back_re, back_im = two_sided(
        far_re * factor[:, None], far_im * factor[:, None], table_re, -table_im
    )
    terms_re = jnp.sum(beam_inphase[None] * back_re + beam_quadrature[None] * back_im, axis=1)
    terms_im = jnp.sum(beam_inphase[None] * back_im - beam_quadrature[None] * back_re, axis=1)
    return (terms_re, terms_im)


def deposit(field, patch, corner):
    width = patch.shape[0]
    current = lax.dynamic_slice(field, (corner[0], corner[1]), (width, width))
    return lax.dynamic_update_slice(field, current + patch, (corner[0], corner[1]))


def local(
    sample_inphase,
    sample_quadrature,
    beam_inphase,
    beam_quadrature,
    recorded_diffraction,
    window_corners,
    filled_tallies,
    absorption_templates,
):
    local_energies = sample_inphase.shape[0]
    side = sample_inphase.shape[1]
    spot_numbering = recorded_diffraction.shape[2]
    width = beam_inphase.shape[-1]
    blocks = lax.axis_size("ea")
    tiles = lax.axis_size("ta")
    tile = lax.axis_index("ta")
    table_re, table_im = dft_tables(width)
    group = 8
    first_slot = jnp.zeros((local_energies,), jnp.int32)
    taken_slots = filled_tallies[:, 0]
    tile_boundary = jnp.full((local_energies,), spot_numbering, jnp.int32)
    gathered_recordings = recorded_diffraction[:, 0]
    pooled_offsets = window_corners[:, 0]

    def lone_wavelength(items):
        o_re, o_im, p_re, p_im, intensity_pool, corner_pool, start, number, split = items
        light_patch = jnp.sum(p_re * p_re + p_im * p_im, axis=0)
        zeros = jnp.zeros((side, side), jnp.float32)

        def advance(index, carry):
            grad_re, grad_im, light = carry
            position = start + index * group + jnp.arange(group, dtype=jnp.int32)
            weight = (position < start + number).astype(jnp.float32)
            source = jnp.where(position < split, position, spot_numbering + position - split)
            source = jnp.clip(source, 0, intensity_pool.shape[0] - 1)
            corners = corner_pool[source]
            terms_re, terms_im = slot_terms(
                o_re, o_im, p_re, p_im, intensity_pool[source], corners, weight, table_re, table_im
            )
            for member in range(group):
                grad_re = deposit(grad_re, terms_re[member], corners[member])
                grad_im = deposit(grad_im, terms_im[member], corners[member])
                light = deposit(light, light_patch * weight[member], corners[member])
            return (grad_re, grad_im, light)

        rounds = (number + group - 1) // group
        return lax.fori_loop(0, rounds, advance, (zeros, zeros, zeros))

    grad_re, grad_im, light = lax.map(
        lone_wavelength,
        (
            sample_inphase,
            sample_quadrature,
            beam_inphase,
            beam_quadrature,
            gathered_recordings,
            pooled_offsets,
            first_slot,
            taken_slots,
            tile_boundary,
        ),
    )

    def shares(field):
        return field.reshape(local_energies, blocks, tiles, -1)

    summed = lax.psum_scatter(
        jnp.stack([shares(grad_re), shares(grad_im), shares(light)]),
        "ta",
        scatter_dimension=3,
        tiled=True,
    )
    light_share = summed[2]
    own_re = lax.dynamic_slice_in_dim(shares(sample_inphase), tile, 1, 2)
    own_im = lax.dynamic_slice_in_dim(shares(sample_quadrature), tile, 1, 2)
    revised_inphase = own_re - summed[0] / (light_share + REGULARIZER)
    revised_quadrature = own_im - summed[1] / (light_share + REGULARIZER)
    spectra = jnp.stack([revised_inphase, revised_quadrature])[:, :, :, 0, :]
    gram = jnp.dot(absorption_templates, absorption_templates.T, precision=HIGHEST_PRECISION)
    factor_low = jnp.linalg.cholesky(gram)
    project = jax.scipy.linalg.cho_solve((factor_low, True), absorption_templates)
    values = lax.all_to_all(spectra, "ea", split_axis=2, concat_axis=1, tiled=True)[:, :, 0, :]
    coefs = jnp.einsum("ke,cen->ckn", project, values, precision=HIGHEST_PRECISION)
    fitted_here = jnp.einsum(
        "ke,ckn->cen", absorption_templates, coefs, precision=HIGHEST_PRECISION
    )
    returned = lax.all_to_all(
        fitted_here[:, :, None, :], "ea", split_axis=1, concat_axis=2, tiled=True
    )
    coef_local = coefs[:, :, None, :]
    return (returned[:, :, :, None, :], coef_local[:, :, 0, :])


def solution(mesh):
    in_specs = (
        P("ea", None, None),
        P("ea", None, None),
        P("ea", None, None, None),
        P("ea", None, None, None),
        P("ea", "ta", None, None, None),
        P("ea", "ta", None, None),
        P("ea", "ta"),
        P(),
    )
    out_specs = (P(None, "ea", None, "ta", None), P(None, None, ("ea", "ta")))
    return jax.shard_map(local, mesh=mesh, in_specs=in_specs, out_specs=out_specs, check_vma=False)
```

profile of v0, /device:TPU:0, one launch (start us, length us, event | category | flops | bytes accessed | tf_op | source)
XLA Modules:
  0.0 2008.1 jit_solution(17726228378883198196)
XLA Ops:
  7.3 1700.3 %while.94 = (s32[]{:T(128)}, f32[8,256,256]{2,1,0:T(8,128)}, f32[8,256,256]{2,1,0:T(8,128)}, f32[8,256,256]{2,1,0:T(8,128)}, s32[8]{0:T(128)}, /*index=5*/s32[8,...) while((s32[]{:T(128)}, f32[8,256,256]{2,1,0:T(8,128)}, ...), condition=%wide.region_7.8_spmd.clone.clone, body=%wide.region_0.7_spmd.clone.clone.sunk | while | flops 151982224 | bytes 8716642 | solution.py:123
  14.0 108.0 %while.95 = (s32[]{:T(128)}, f32[256,256]{1,0:T(8,128)S(1)}, f32[256,256]{1,0:T(8,128)S(1)}, f32[256,256]{1,0:T(8,128)S(1)}, s32[]{:T(128)}, /*index=5*/s32[16,2...) while((s32[]{:T(128)}, f32[256,256]{1,0:T(8,128)S(1)}, ...), condition=%wide.region_6.6_spmd.clone, body=%wide.region_2.5_spmd.clone.sunk | while | flops 151921792 | bytes 5110015 | solution.py:121
  60.6 15.4 while.97
  130.3 219.8 %while.95 = (s32[]{:T(128)}, f32[256,256]{1,0:T(8,128)S(1)}, f32[256,256]{1,0:T(8,128)S(1)}, f32[256,256]{1,0:T(8,128)S(1)}, s32[]{:T(128)}, /*index=5*/s32[16,2...) while((s32[]{:T(128)}, f32[256,256]{1,0:T(8,128)S(1)}, ...), condition=%wide.region_6.6_spmd.clone, body=%wide.region_2.5_spmd.clone.sunk | while | flops 151921792 | bytes 5110015 | solution.py:121
  177.7 15.4 while.97
  193.1 15.4 while.96
  287.8 15.4 while.97
  303.2 15.4 while.96
  358.4 219.3 %while.95 = (s32[]{:T(128)}, f32[256,256]{1,0:T(8,128)S(1)}, f32[256,256]{1,0:T(8,128)S(1)}, f32[256,256]{1,0:T(8,128)S(1)}, s32[]{:T(128)}, /*index=5*/s32[16,2...) while((s32[]{:T(128)}, f32[256,256]{1,0:T(8,128)S(1)}, ...), condition=%wide.region_6.6_spmd.clone, body=%wide.region_2.5_spmd.clone.sunk | while | flops 151921792 | bytes 5110015 | solution.py:121
  420.6 15.4 while.96
  514.5 15.4 while.97
  529.9 15.4 while.96
  586.0 216.0 %while.95 = (s32[]{:T(128)}, f32[256,256]{1,0:T(8,128)S(1)}, f32[256,256]{1,0:T(8,128)S(1)}, f32[256,256]{1,0:T(8,128)S(1)}, s32[]{:T(128)}, /*index=5*/s32[16,2...) while((s32[]{:T(128)}, f32[256,256]{1,0:T(8,128)S(1)}, ...), condition=%wide.region_6.6_spmd.clone, body=%wide.region_2.5_spmd.clone.sunk | while | flops 151921792 | bytes 5110015 | solution.py:121
  648.0 15.4 while.96
  740.6 15.4 while.97
  756.0 15.4 while.96
  810.3 216.4 %while.95 = (s32[]{:T(128)}, f32[256,256]{1,0:T(8,128)S(1)}, f32[256,256]{1,0:T(8,128)S(1)}, f32[256,256]{1,0:T(8,128)S(1)}, s32[]{:T(128)}, /*index=5*/s32[16,2...) while((s32[]{:T(128)}, f32[256,256]{1,0:T(8,128)S(1)}, ...), condition=%wide.region_6.6_spmd.clone, body=%wide.region_2.5_spmd.clone.sunk | while | flops 151921792 | bytes 5110015 | solution.py:121
  856.8 15.4 while.97
  1034.9 220.2 %while.95 = (s32[]{:T(128)}, f32[256,256]{1,0:T(8,128)S(1)}, f32[256,256]{1,0:T(8,128)S(1)}, f32[256,256]{1,0:T(8,128)S(1)}, s32[]{:T(128)}, /*index=5*/s32[16,2...) while((s32[]{:T(128)}, f32[256,256]{1,0:T(8,128)S(1)}, ...), condition=%wide.region_6.6_spmd.clone, body=%wide.region_2.5_spmd.clone.sunk | while | flops 151921792 | bytes 5110015 | solution.py:121
  1082.3 15.4 while.97
  1097.7 15.4 while.96
  1207.9 15.4 while.96
  1263.4 217.2 %while.95 = (s32[]{:T(128)}, f32[256,256]{1,0:T(8,128)S(1)}, f32[256,256]{1,0:T(8,128)S(1)}, f32[256,256]{1,0:T(8,128)S(1)}, s32[]{:T(128)}, /*index=5*/s32[16,2...) while((s32[]{:T(128)}, f32[256,256]{1,0:T(8,128)S(1)}, ...), condition=%wide.region_6.6_spmd.clone, body=%wide.region_2.5_spmd.clone.sunk | while | flops 151921792 | bytes 5110015 | solution.py:121
  1419.2 15.4 while.97
  1434.6 15.4 while.96
  1488.9 216.7 %while.95 = (s32[]{:T(128)}, f32[256,256]{1,0:T(8,128)S(1)}, f32[256,256]{1,0:T(8,128)S(1)}, f32[256,256]{1,0:T(8,128)S(1)}, s32[]{:T(128)}, /*index=5*/s32[16,2...) while((s32[]{:T(128)}, f32[256,256]{1,0:T(8,128)S(1)}, ...), condition=%wide.region_6.6_spmd.clone, body=%wide.region_2.5_spmd.clone.sunk | while | flops 151921792 | bytes 5110015 | solution.py:121
  1535.8 15.4 while.97
  1551.2 15.4 while.96
  1659.7 15.4 while.96
  1736.6 130.3 %all-reduce.3.cloned.1.call-done = f32[3,8,16,2,2048]{4,1,2,3,0:T(8,128)} async-done(((f32[3,8,16,2,2048]{4,1,2,3,0:T(8,128)}), f32[3,8,16,2,2048]{4,1,2,3,0:T(8,128)}) %all-reduce.3.cloned.1.call-update) | async-done | bytes 6291472
  1890.1 38.7 %all-to-all-done = f32[2,8,16,2048]{3,1,0,2:T(8,128)S(1)} async-done(((f32[2,8,16,2048]{3,1,0,2:T(8,128)}), f32[2,8,16,2048]{3,1,0,2:T(8,128)S(1)}, u32[]{:S(2)}, u32[]{:S(2)}) %all-to-all-start) | async-done | bytes 2097184 | tf_op jit(solution)/shard_map/all_to_all | solution.py:156
  1937.7 58.6 %all_to_all.30 = f32[2,128,1,2048]{3,0,2,1:T(2,128)S(1)} all-to-all(f32[2,128,1,2048]{3,0,2,1:T(2,128)S(1)} %copy.116), channel_id=1, replica_groups=mesh['ea'=16,'ta'=2] {'ea'}, dimensions={1} | all-to-all | bytes 4194304 | tf_op jit(solution)/shard_map/all_to_all | solution.py:161
  (2050 shorter events, 1457.3 us)
Async XLA Ops:
  7.2 1878.3 %copy-start = (f32[16,128]{1,0:T(8,128)S(1)}, f32[16,128]{1,0:T(8,128)}, u32[]{:S(2)}) copy-start(f32[16,128]{1,0:T(8,128)} %param.19) | copy-start | bytes 24580
  7.2 1859.8 %all-reduce.3.cloned.1.call-start = ((), (), s32[]{:S(2)}) async-start(), calls=%async_computation.2 | async-start | bytes 12582912
  1711.1 3.7 copy-start.3
  1729.5 1.6 copy-start.1
  1733.4 2.6 copy-start.5
  1866.9 2.9 copy-start.2
  1878.7 50.0 %all-to-all-start = ((f32[2,8,16,2048]{3,1,0,2:T(8,128)}), f32[2,8,16,2048]{3,1,0,2:T(8,128)S(1)}, u32[]{:S(2)}, u32[]{:S(2)}) async-start(f32[2,8,16,2048]{3,1,0,2:T(8,128)} %bitcast.407), calls=%async_computation | async-start | bytes 4194304 | tf_op jit(solution)/shard_map/all_to_all | solution.py:156
  1929.9 7.7 copy-start.4
Sparse Core Ops, SparseCore 0:
  1729.7 137.2 all-reduce.2
where the time goes:
time: 2020 us; the launch traced here: 2010 us
  local copies, waits for them, and re-layouts  954 us (47%)
  loops' own time  463 us (23%)
  matrix products  198 us (10%)
  waiting for transfers between devices  169 us (8%)
  other arithmetic  144 us (7%)
  blocking collectives  58.6 us (3%)
    gather x720, local copies, waits for them, and re-layouts  461 us
    another operation x8, loops' own time, lone_wavelength(): return lax.fori_loop(0, rounds, advance, (zeros, zeros, zeros))  456 us
    dynamic_update_slice x360, local copies, waits for them, and re-layouts, deposit(): lax.dynamic_update_slice(field, current + patch, (corner[0], corner[1]))  364 us
    unnamed x2, waiting for transfers between devices  130 us
    add x345, other arithmetic, deposit(): current + patch  106 us
    all_to_all x1, blocking collectives, local(): lax.all_to_all(fitted_here[:, :, None, :], 'ea', split_axis=1, concat_axi...  58.6 us
  transfers between devices with their start and end apart: 2, of which 2 were waited for; matrix products, arithmetic and copies ran while one was open for 1% of the time, Pallas kernels for 0%

commit v1 on v0

v1 whole, which is shorter than its diff:
```python
import functools

import jax
import jax.numpy as jnp
import numpy as np
from jax import lax
from jax.experimental import pallas as pl
from jax.experimental.pallas import tpu as pltpu
from jax.sharding import PartitionSpec as P

HIGHEST = lax.Precision.HIGHEST
FLOOR_POWER = 0.5
REGULARIZER = 1.0
LANES = 128
SUBS = 8


def split_bf16(x):
    hi = x.astype(jnp.bfloat16)
    lo = (x - hi.astype(jnp.float32)).astype(jnp.bfloat16)
    return hi, lo


def transform_tables(width):
    fold = LANES // width
    i = np.arange(LANES) // width
    k = np.arange(LANES) % width
    phase = np.outer(i, i) / fold + np.outer(k, k) / width
    m = np.exp(-2j * np.pi * phase) / width
    real = np.block([[m.real, m.imag], [-m.imag, m.real]])
    q = np.arange(SUBS)
    tw = np.exp(-2j * np.pi * np.outer(q, i) / width)
    tw = np.concatenate([tw.real, tw.imag]).astype(np.float32)

    def halves(a):
        hi = a.astype(jnp.bfloat16)
        lo = (a - hi.astype(np.float64)).astype(jnp.bfloat16)
        return np.stack([hi, lo])

    return halves(real), halves(real.T.copy()), tw


def fft8(re, im, sign):
    def butterfly(a, b):
        return (a[0] + b[0], a[1] + b[1]), (a[0] - b[0], a[1] - b[1])

    def turn(a):
        return (-a[1], a[0]) if sign > 0 else (a[1], -a[0])

    h = np.float32(np.sqrt(0.5))

    def eighth(a):
        if sign > 0:
            return ((a[0] - a[1]) * h, (a[0] + a[1]) * h)
        return ((a[0] + a[1]) * h, (a[1] - a[0]) * h)

    def fft4(x):
        s0, d0 = butterfly(x[0], x[2])
        s1, d1 = butterfly(x[1], x[3])
        d1 = turn(d1)
        y0, y2 = butterfly(s0, s1)
        y1, y3 = butterfly(d0, d1)
        return [y0, y1, y2, y3]

    x = list(zip(re, im))
    e = fft4(x[0::2])
    o = fft4(x[1::2])
    o = [o[0], eighth(o[1]), turn(o[2]), turn(eighth(o[3]))]
    pairs = [butterfly(e[n], o[n]) for n in range(4)]
    out = [p[0] for p in pairs] + [p[1] for p in pairs]
    return [y[0] for y in out], [y[1] for y in out]


def step_kernel(
    n_e, spots, used, modes, width,
    first_ref, own_corner, par_corner, own_count,
    re0, re1, im0, im1, pr_ref, pi_ref, own_rec, par_rec, wf_ref, wb_ref, tw_ref,
    out_ref,
    rec, patch_re, patch_im, root, work, acc, light_row, sem,
):
    fold = LANES // width
    groups = used // SUBS
    per_group = modes * SUBS
    rows = groups * per_group
    first = first_ref[0]
    copies = [
        pltpu.make_async_copy(own_rec.at[pl.ds(first, n_e)], rec.at[:, pl.ds(0, spots)], sem.at[0]),
        pltpu.make_async_copy(par_rec, rec.at[:, pl.ds(spots, spots)], sem.at[1]),
    ]
    for c in copies:
        c.start()
    lane = lax.broadcasted_iota(jnp.int32, (SUBS, LANES), 1)
    block = lane // width
    acc[...] = jnp.zeros_like(acc)

    def place(e, index):
        count = own_count[first + e]
        mine = index < count
        slot = jnp.where(mine, index, index - count)
        slot = jnp.clip(slot, 0, spots - 1)
        at = ((first + e) * spots + slot) * 2
        row = jnp.where(mine, own_corner[at], par_corner[at])
        col = jnp.where(mine, own_corner[at + 1], par_corner[at + 1])
        return jnp.where(mine, slot, slot + spots), row, col

    def merge(parts):
        out = parts[0]
        for n in range(1, fold):
            out = jnp.where(block == n, parts[n], out)
        return out

    def extract(n, carry):
        e, g = n // groups, n % groups
        for s in range(SUBS):
            _, row, col = place(e, g * SUBS + s)
            low = lane >= col
            to = pl.multiple_of((n * SUBS + s) * SUBS, SUBS)
            for left, right, dst in ((re0, re1, patch_re), (im0, im1, patch_im)):
                parts = []
                for i in range(fold):
                    at = pl.ds(row + i, SUBS, stride=fold)
                    v = jnp.where(low, left[e, at, :], right[e, at, :])
                    parts.append(pltpu.roll(v, (i * width - col) & (LANES - 1), 1))
                dst[pl.ds(to, SUBS), :] = merge(parts)
        return carry

    lax.fori_loop(0, n_e * groups, extract, 0)
    for c in copies:
        c.wait()

    def roots(n, carry):
        e, g = n // groups, n % groups
        for s in range(SUBS):
            slot, _, _ = place(e, g * SUBS + s)
            to = pl.multiple_of((n * SUBS + s) * SUBS, SUBS)
            v = jnp.concatenate(
                [rec[e, slot, r * SUBS:(r + 1) * SUBS, :] for r in range(fold)], axis=1
            )
            root[pl.ds(to, SUBS), :] = jnp.sqrt(v)
        return carry

    lax.fori_loop(0, n_e * groups, roots, 0)

    def row_of(ref, *index):
        return jnp.broadcast_to(ref[index], (SUBS, LANES))

    def multiply(w_ref):
        for q in range(SUBS):
            hi, lo = split_bf16(work[q])
            dot = functools.partial(jnp.dot, preferred_element_type=jnp.float32)
            work[q] = dot(hi, w_ref[0]) + dot(lo, w_ref[0]) + dot(hi, w_ref[1])

    def energy(e, carry):
        def forward(g, carry):
            base = (e * groups + g) * SUBS * SUBS
            o_re, o_im = [], []
            for t in range(SUBS):
                at = pl.ds(base + t, SUBS, stride=SUBS)
                o_re.append(patch_re[at, :])
                o_im.append(patch_im[at, :])
            for m in range(modes):
                x_re, x_im = [], []
                for t in range(SUBS):
                    p_re = row_of(pr_ref, e, m, pl.ds(t, 1), slice(None))
                    p_im = row_of(pi_ref, e, m, pl.ds(t, 1), slice(None))
                    x_re.append(p_re * o_re[t] - p_im * o_im[t])
                    x_im.append(p_re * o_im[t] + p_im * o_re[t])
                y_re, y_im = fft8(x_re, x_im, -1)
                to = pl.ds(pl.multiple_of(g * per_group + m * SUBS, SUBS), SUBS)
                for q in range(SUBS):
                    a, b = y_re[q], y_im[q]
                    if q:
                        c = row_of(tw_ref, pl.ds(q, 1), slice(None))
                        d = row_of(tw_ref, pl.ds(SUBS + q, 1), slice(None))
                        a, b = a * c - b * d, a * d + b * c
                    work[q, to, 0:LANES] = a
                    work[q, to, LANES:2 * LANES] = b
            return carry

        lax.fori_loop(0, groups, forward, 0)
        multiply(wf_ref)

        def scale(g, carry):
            base = (e * groups + g) * SUBS * SUBS
            for q in range(SUBS):
                tos = [
                    pl.ds(pl.multiple_of(g * per_group + m * SUBS, SUBS), SUBS)
                    for m in range(modes)
                ]
                f = [(work[q, to, 0:LANES], work[q, to, LANES:2 * LANES]) for to in tos]
                power = f[0][0] * f[0][0] + f[0][1] * f[0][1]
                for a, b in f[1:]:
                    power = power + a * a + b * b
                sq = root[pl.ds(base + q, SUBS, stride=SUBS), :]
                factor = 1.0 - sq * lax.rsqrt(jnp.maximum(power, FLOOR_POWER))
                for to, (a, b) in zip(tos, f):
                    work[q, to, 0:LANES] = a * factor
                    work[q, to, LANES:2 * LANES] = b * factor
            return carry

        lax.fori_loop(0, groups, scale, 0)
        multiply(wb_ref)

        light = jnp.zeros((SUBS, LANES), jnp.float32)
        for m in range(modes):
            a, b = pr_ref[e, m], pi_ref[e, m]
            light = light + a * a + b * b

        def backward(g, carry):
            base = (e * groups + g) * SUBS * SUBS
            t_re = [None] * SUBS
            t_im = [None] * SUBS
            for m in range(modes):
                frm = pl.ds(pl.multiple_of(g * per_group + m * SUBS, SUBS), SUBS)
                x_re, x_im = [], []
                for q in range(SUBS):
                    a, b = work[q, frm, 0:LANES], work[q, frm, LANES:2 * LANES]
                    if q:
                        c = row_of(tw_ref, pl.ds(q, 1), slice(None))
                        d = row_of(tw_ref, pl.ds(SUBS + q, 1), slice(None))
                        a, b = a * c + b * d, b * c - a * d
                    x_re.append(a)
                    x_im.append(b)
                y_re, y_im = fft8(x_re, x_im, 1)
                for t in range(SUBS):
                    p_re = row_of(pr_ref, e, m, pl.ds(t, 1), slice(None))
                    p_im = row_of(pi_ref, e, m, pl.ds(t, 1), slice(None))
                    a = p_re * y_re[t] + p_im * y_im[t]
                    b = p_re * y_im[t] - p_im * y_re[t]
                    t_re[t] = a if m == 0 else t_re[t] + a
                    t_im[t] = b if m == 0 else t_im[t] + b
            for t in range(SUBS):
                at = pl.ds(base + t, SUBS, stride=SUBS)
                patch_re[at, :] = t_re[t]
                patch_im[at, :] = t_im[t]
            for s in range(SUBS):
                _, row, col = place(e, g * SUBS + s)
                frm = pl.ds(pl.multiple_of(base + s * SUBS, SUBS), SUBS)
                terms = (patch_re[frm, :], patch_im[frm, :], light)
                away = [lane + h * LANES - col for h in range(2)]
                inside = [(a >= 0) & (a < width) for a in away]
                for i in range(fold):
                    at = pl.ds(row + i, SUBS, stride=fold)
                    for n, term in enumerate(terms):
                        v = pltpu.roll(term, (col - i * width) & (LANES - 1), 1)
                        for h in range(2):
                            acc[n, h, e, at, :] = acc[n, h, e, at, :] + jnp.where(inside[h], v, 0.0)
            return carry

        lax.fori_loop(0, groups, backward, 0)
        return carry

    lax.fori_loop(0, n_e, energy, 0)

    side = re0.shape[1]

    def finish(n, carry):
        at = pl.ds(pl.multiple_of(n * SUBS, SUBS), SUBS)
        for e in range(n_e):
            for h, (o_re, o_im) in enumerate(((re0, im0), (re1, im1))):
                cols = slice(h * LANES, (h + 1) * LANES)
                share = 1.0 / (acc[2, h, e, at, :] + REGULARIZER)
                out_ref[n, 0, e, :, cols] = o_re[e, at, :] - acc[0, h, e, at, :] * share
                out_ref[n, 1, e, :, cols] = o_im[e, at, :] - acc[1, h, e, at, :] * share
        return carry

    lax.fori_loop(0, side // SUBS, finish, 0)


def gradient_step(objects, beams, own_rec, par_rec, own_corner, par_corner, own_count, first, n_e, used):
    o_re, o_im = objects
    local, side, _ = o_re.shape
    modes, width = beams[0].shape[1], beams[0].shape[-1]
    spots = own_rec.shape[1]
    flat = width * width // LANES
    assert flat == SUBS and side == 2 * LANES and used % SUBS == 0
    wf, wb, tw = transform_tables(width)
    shaped = [b.reshape(local, modes, flat, LANES) for b in beams]
    part = lambda i, f, *_: (f[0] // n_e, 0, 0, 0)
    half = [pl.BlockSpec((n_e, side, LANES), lambda i, f, *_, h=h: (f[0] // n_e, 0, h)) for h in range(2)]
    beam_spec = pl.BlockSpec((n_e, modes, flat, LANES), part)
    whole = pl.BlockSpec(memory_space=pltpu.VMEM)
    rows = used * modes
    n = n_e * used * SUBS
    return pl.pallas_call(
        functools.partial(step_kernel, n_e, spots, used, modes, width),
        out_shape=jax.ShapeDtypeStruct((side // SUBS, 2, n_e, SUBS, side), jnp.float32),
        grid_spec=pltpu.PrefetchScalarGridSpec(
            num_scalar_prefetch=4,
            grid=(1,),
            in_specs=[
                half[0], half[1], half[0], half[1], beam_spec, beam_spec,
                pl.BlockSpec(memory_space=pl.ANY), pl.BlockSpec(memory_space=pl.ANY),
                whole, whole, whole,
            ],
            out_specs=pl.BlockSpec(
                (side // SUBS, 2, n_e, SUBS, side), lambda i, *_: (0, 0, 0, 0, 0)
            ),
            scratch_shapes=[
                pltpu.VMEM((n_e, 2 * spots, width, width), jnp.float32),
                pltpu.VMEM((n, LANES), jnp.float32),
                pltpu.VMEM((n, LANES), jnp.float32),
                pltpu.VMEM((n, LANES), jnp.float32),
                pltpu.VMEM((SUBS, rows, 2 * LANES), jnp.float32),
                pltpu.VMEM((3, 2, n_e, side, LANES), jnp.float32),
                pltpu.VMEM((SUBS, LANES), jnp.float32),
                pltpu.SemaphoreType.DMA((2,)),
            ],
        ),
        name="gradient_step",
    )(
        first, own_corner, par_corner, own_count,
        o_re, o_re, o_im, o_im, *shaped, own_rec, par_rec, jnp.asarray(wf), jnp.asarray(wb), jnp.asarray(tw),
    )


def local(
    sample_inphase,
    sample_quadrature,
    beam_inphase,
    beam_quadrature,
    recorded_diffraction,
    window_corners,
    filled_tallies,
    absorption_templates,
):
    local_energies = sample_inphase.shape[0]
    side = sample_inphase.shape[1]
    spots = recorded_diffraction.shape[2]
    blocks = lax.axis_size("ea")
    tiles = lax.axis_size("ta")
    tile = lax.axis_index("ta")
    swap = [(0, 1), (1, 0)]
    assert tiles == 2
    used = spots * 3 // 2
    divided = local_energies % tiles == 0
    n_e = local_energies // tiles if divided else local_energies
    own_rec = recorded_diffraction[:, 0]
    first = tile * n_e if divided else jnp.zeros((), jnp.int32)
    give = lax.dynamic_slice_in_dim(own_rec, (1 - tile) * n_e, n_e, 0) if divided else own_rec
    par_rec = lax.ppermute(give, "ta", swap)
    own_corner = window_corners.reshape(-1)
    par_corner = lax.ppermute(own_corner, "ta", swap)
    stepped = gradient_step(
        (sample_inphase, sample_quadrature),
        (beam_inphase, beam_quadrature),
        own_rec,
        par_rec,
        own_corner,
        par_corner,
        filled_tallies.reshape(-1),
        first.astype(jnp.int32)[None],
        n_e,
        used,
    )
    gram = jnp.dot(absorption_templates, absorption_templates.T, precision=HIGHEST)
    factor_low = jnp.linalg.cholesky(gram)
    project = jax.scipy.linalg.cho_solve((factor_low, True), absorption_templates)
    edges = project.shape[0]
    pix = side * side // (blocks * tiles)
    if divided and pix == SUBS * side:
        got = lax.all_to_all(stepped, ("ea", "ta"), 0, 0, tiled=True)
        got = got.reshape(blocks * tiles, 2, n_e, pix)
        values = jnp.moveaxis(got, 1, 0).reshape(2, -1, pix)
    else:
        if divided:
            parts = blocks * tiles
            flat = jnp.moveaxis(stepped, 0, 2).reshape(2, n_e, parts, pix)
            got = lax.all_to_all(flat, ("ea", "ta"), 2, 1, tiled=True)
        else:
            flat = jnp.moveaxis(stepped, 0, 2).reshape(2, n_e, blocks, tiles, pix)
            flat = lax.dynamic_index_in_dim(flat, tile, 3, keepdims=False)
            got = lax.all_to_all(flat, "ea", 2, 1, tiled=True)
        values = got.reshape(2, -1, pix)
    coefs = jnp.einsum("ke,cen->ckn", project, values, precision=HIGHEST)
    fitted_here = jnp.einsum("ke,ckn->cen", absorption_templates, coefs, precision=HIGHEST)
    returned = lax.all_to_all(
        fitted_here[:, :, None, :], "ea", split_axis=1, concat_axis=2, tiled=True
    )
    return (returned[:, :, :, None, :], coefs)


def solution(mesh):
    in_specs = (
        P("ea", None, None),
        P("ea", None, None),
        P("ea", None, None, None),
        P("ea", None, None, None),
        P("ea", "ta", None, None, None),
        P("ea", "ta", None, None),
        P("ea", "ta"),
        P(),
    )
    out_specs = (P(None, "ea", None, "ta", None), P(None, None, ("ea", "ta")))
    return jax.shard_map(local, mesh=mesh, in_specs=in_specs, out_specs=out_specs, check_vma=False)
```

time: 2020 us -> 156 us (0.08)
  local copies, waits for them, and re-layouts: 954 us -> 19 us
  loops' own time: 463 us -> 0 us
  matrix products: 198 us -> 6.43 us
  other arithmetic: 144 us -> 4.02 us
  waiting for transfers between devices: 169 us -> 44.5 us
    gather x750 -> x0, local copies, waits for them, and re-layouts: 478 us -> none
    another operation x39 -> x0, loops' own time: 463 us -> none  [the longest x8 456 us: lone_wavelength(): return lax.fori_loop(0, rounds, advance, (zeros, zeros, zeros))]
    dynamic_update_slice x376 -> x0, local copies, waits for them, and re-layouts: 377 us -> none  [the longest x360 364 us: deposit(): lax.dynamic_update_slice(field, current + patch, (corner[0], corner[1]))]
    dot_general x243 -> x3, matrix products: 198 us -> 6.09 us  [the longest x1 4.76 us: local(): jnp.einsum('ke,ckn->cen', absorption_templates, coefs, precision=HIGHEST)]
    unnamed x2 -> x0, waiting for transfers between devices: 130 us -> none
    add x345 -> x0, other arithmetic: 106 us -> none  [deposit(): current + patch]
    squeeze x33 -> x0, local copies, waits for them, and re-layouts: 31.4 us -> none  [the longest x32 28.9 us: local(): lax.map(lone_wavelength, (sample_inphase, sample_quadrature, beam_inphase...]
    slice x31 -> x0, local copies, waits for them, and re-layouts: 23.7 us -> none  [the longest x15 10.5 us: deposit(): current = lax.dynamic_slice(field, (corner[0], corner[1]), (width, width))]
  transfers between devices with their start and end apart: 2 -> 3, of which waited for: 2 -> 2; matrix products, arithmetic and copies ran while one was open for 1% -> 4% of each run, Pallas kernels for 0% -> 0%
where the time goes in v1:
time: 156 us
  blocking collectives  53.9 us (35%)
  waiting for transfers between devices  44.5 us (29%)
  Pallas kernels  19.3 us (12%)
  local copies, waits for them, and re-layouts  19 us (12%)
  starting transfers between devices  7.84 us (5%)
  matrix products  6.43 us (4%)
  other arithmetic  4.02 us (3%)
    all_to_all x1, blocking collectives, local(): lax.all_to_all(fitted_here[:, :, None, :], 'ea', split_axis=1, concat_axi...  53.9 us
    all_to_all x1, waiting for transfers between devices, local(): got = lax.all_to_all(stepped, ('ea', 'ta'), 0, 0, tiled=True)  44.1 us
    pallas_call x1, Pallas kernels, gradient_step(): pl.pallas_call(functools.partial(step_kernel, n_e, spots, used, modes, wi...  19.3 us
    all_to_all x1, starting transfers between devices, local(): got = lax.all_to_all(stepped, ('ea', 'ta'), 0, 0, tiled=True)  7.19 us
    dot_general x1, matrix products, local(): jnp.einsum('ke,ckn->cen', absorption_templates, coefs, precision=HIGHEST)  4.76 us
    unnamed x18, local copies, waits for them, and re-layouts  4.6 us
    transpose x1, local copies, waits for them, and re-layouts, local(): values = jnp.moveaxis(got, 1, 0).reshape(2, -1, pix)  3.19 us
  transfers between devices with their start and end apart: 3, of which 2 were waited for; matrix products, arithmetic and copies ran while one was open for 4% of the time, Pallas kernels for 0%

profile of v1, /device:TPU:0, one launch (start us, length us, event | category | flops | bytes accessed | tf_op | source)
XLA Modules:
  0.0 155.9 jit_solution(1155105026926581668)
XLA Ops:
  0.6 0.0 copy-start
  0.7 1.4 dynamic-slice_bitcast_fusion
  2.1 0.6 collective-permute-start.1
  2.6 0.1 copy.21
  2.7 0.1 reshape.37.own_corner
  2.9 0.1 collective-permute-start
  3.0 0.8 reshape.39.pr_ref
  3.8 0.8 reshape.40.pi_ref
  4.5 0.4 collective-permute-done.par_corner
  4.9 0.0 collective-permute-done.1.par_rec
  4.9 0.6 copy-done.7
  5.5 0.4 copy-done.1
  5.9 19.3 %gradient_step.1 = f32[32,2,4,8,256]{4,3,2,1,0:T(8,128)} custom-call(s32[1]{0:T(128)} %bitcast.first_ref, s32[256]{0:T(256)} %copy-done.6, s32[256]{0:T(256)} %copy-done.7, s32[8]{0:T(128)} %bitcast.53, f32[8,256,256]{2,1,0:T(8,128)} %re1.1, f32[8,256,256]{2,1,0:T(8,128)} %re1.1, f32[8,256,256]{2,1,0:T(8,128)} %im1.1, f32[8,256,256]{2,1,0:T(8,128)} %im1.1, ...), custom_call_target="tpu_custom_call" | custom-call | tf_op jit(solution)/shard_map/gradient_step/pallas_call | solution.py:285
  25.2 7.2 %all-to-all-start = ((f32[32,2,4,8,256]{4,3,2,1,0:T(8,128)}), f32[32,2,4,8,256]{4,3,2,1,0:T(8,128)S(1)}, u32[]{:S(2)}, u32[]{:S(2)}) async-start(f32[32,2,4,8,256]{4,3,2,1,0:T(8,128)} %gradient_step.1), calls=%async_computation | async-start | bytes 4194304 | tf_op jit(solution)/shard_map/all_to_all | solution.py:362
  32.4 0.1 fusion.6
  32.6 0.1 copy.23
  32.6 1.5 cholesky.16
  34.1 0.6 compare_reduce_fusion
  34.8 0.6 fusion
  35.4 1.2 custom-call.10
  36.7 0.2 fusion.3
  36.9 0.1 convolution_bitcast_fusion.2
  37.0 44.1 %all-to-all-done = f32[32,2,4,8,256]{4,3,2,1,0:T(8,128)S(1)} async-done(((f32[32,2,4,8,256]{4,3,2,1,0:T(8,128)}), f32[32,2,4,8,256]{4,3,2,1,0:T(8,128)S(1)}, u32[]{:S(2)}, u32[]{:S(2)}) %all-to-all-start) | async-done | bytes 2097184 | tf_op jit(solution)/shard_map/all_to_all | solution.py:362
  81.2 2.0 %reshape.41 = f32[32,2,4,2048]{3,2,1,0:T(4,128)} reshape(f32[32,2,4,8,256]{4,3,2,1,0:T(8,128)S(1)} %all-to-all-done) | data formatting | bytes 4194304 | tf_op jit(solution)/shard_map/reshape | solution.py:363
  83.1 3.2 %copy.22 = f32[2,32,4,2048]{3,2,1,0:T(4,128)} copy(f32[2,32,4,2048]{3,2,0,1:T(4,128)} %bitcast.50) | data formatting | bytes 4194304 | tf_op jit(solution)/shard_map/transpose | solution.py:364
  86.3 2.0 %reshape.42 = f32[2,128,2048]{2,1,0:T(8,128)S(1)} reshape(f32[2,32,4,2048]{3,2,1,0:T(4,128)} %copy.22) | data formatting | bytes 4194304 | tf_op jit(solution)/shard_map/reshape | solution.py:364
  88.3 1.2 convolution_bitcast_fusion.1
  89.5 4.8 %convolution_bitcast_fusion = f32[2,128,1,2048]{1,3,0,2:T(8,128)} fusion(f32[2,16,2048]{2,1,0:T(8,128)S(1)} %convolution_bitcast_fusion.1, f32[16,128]{1,0:T(8,128)S(1)} %copy-done), kind=kOutput, calls=%fused_computation | convolution fusion | flops 100663296 | bytes 2367488 | tf_op jit(solution)/shard_map/ke,ckn->cen/dot_general | solution.py:376
  94.3 2.9 %copy.24 = f32[2,128,1,2048]{3,0,2,1:T(2,128)S(1)} copy(f32[2,128,1,2048]{1,3,0,2:T(8,128)} %convolution_bitcast_fusion) | data formatting | bytes 4194304 | tf_op jit(solution)/shard_map/broadcast_in_dim | solution.py:378
  97.2 53.9 %all_to_all.20 = f32[2,128,1,2048]{3,0,2,1:T(2,128)S(1)} all-to-all(f32[2,128,1,2048]{3,0,2,1:T(2,128)S(1)} %copy.24), channel_id=1, replica_groups=mesh['ea'=16,'ta'=2] {'ea'}, dimensions={1} | all-to-all | bytes 4194304 | tf_op jit(solution)/shard_map/all_to_all | solution.py:377
  151.2 1.2 copy.28
  152.4 3.5 %copy.26 = f32[2,8,16,1,2048]{4,3,2,1,0:T(1,128)} copy(f32[2,8,16,1,2048]{4,1,2,0,3:T(8,128)S(1)} %bitcast.51) | data formatting | bytes 4194304
  (15 shorter events, 0.1 us)
Async XLA Ops:
  0.6 31.8 %copy-start = (f32[16,128]{1,0:T(8,128)S(1)}, f32[16,128]{1,0:T(8,128)}, u32[]{:S(2)}) copy-start(f32[16,128]{1,0:T(8,128)} %param.18) | copy-start | bytes 24580
  0.6 2.0 %copy-start.5 = (s32[8,1,16,2]{2,3,1,0:T(2,128)S(1)}, s32[8,1,16,2]{2,3,1,0:T(2,128)}, u32[]{:S(2)}) copy-start(s32[8,1,16,2]{2,3,1,0:T(2,128)} %param.16) | copy-start | bytes 3076
  0.7 2.3 %copy-start.3 = (f32[8,3,32,32]{3,2,1,0:T(8,128)S(1)}, f32[8,3,32,32]{3,2,1,0:T(8,128)}, u32[]{:S(2)}) copy-start(f32[8,3,32,32]{3,2,1,0:T(8,128)} %param.13) | copy-start | bytes 294916
  0.7 3.1 %copy-start.4 = (f32[8,3,32,32]{3,2,1,0:T(8,128)S(1)}, f32[8,3,32,32]{3,2,1,0:T(8,128)}, u32[]{:S(2)}) copy-start(f32[8,3,32,32]{3,2,1,0:T(8,128)} %param.14) | copy-start | bytes 294916
  2.1 2.9 %collective-permute-start.1 = (f32[4,16,32,32]{3,2,1,0:T(8,128)S(1)}, f32[4,16,32,32]{3,2,1,0:T(8,128)S(1)}, u32[]{:S(2)}, u32[]{:S(2)}) collective-permute-start(f32[4,16,32,32]{3,2,1,0:T(8,128)S(1)} %dynamic-slice_bitcast_fusion), channel_id=1, source_target_pairs={{0,1},{1,0},{2,3},{3,2},{4,5},{5,4},{6,7},{7,6},{8,9},{9,8},{10,11... | collective-permute-start | bytes 786440 | tf_op jit(solution)/shard_map/ppermute | solution.py:341
  2.9 2.0 %copy-start.6 = (s32[256]{0:T(256)}, s32[256]{0:T(256)S(1)}, u32[]{:S(2)}) copy-start(s32[256]{0:T(256)S(1)} %reshape.37.own_corner) | copy-start | bytes 3076
  2.9 2.0 %collective-permute-start = (s32[256]{0:T(256)S(1)}, s32[256]{0:T(256)S(1)}, u32[]{:S(2)}, u32[]{:S(2)}) collective-permute-start(s32[256]{0:T(256)S(1)} %reshape.37.own_corner), channel_id=1, source_target_pairs={{0,1},{1,0},{2,3},{3,2},{4,5},{5,4},{6,7},{7,6},{8,9},{9,8},{10,11... | collective-permute-start | bytes 3080 | tf_op jit(solution)/shard_map/ppermute | solution.py:343
  4.9 0.6 copy-start.7
  4.9 1.0 copy-start.1
  25.2 55.9 %all-to-all-start = ((f32[32,2,4,8,256]{4,3,2,1,0:T(8,128)}), f32[32,2,4,8,256]{4,3,2,1,0:T(8,128)S(1)}, u32[]{:S(2)}, u32[]{:S(2)}) async-start(f32[32,2,4,8,256]{4,3,2,1,0:T(8,128)} %gradient_step.1), calls=%async_computation | async-start | bytes 4194304 | tf_op jit(solution)/shard_map/all_to_all | solution.py:362
  89.5 7.7 %copy-start.2 = (f32[2,16,2048]{2,1,0:T(8,128)}, f32[2,16,2048]{2,1,0:T(8,128)S(1)}, u32[]{:S(2)}) copy-start(f32[2,16,2048]{2,1,0:T(8,128)S(1)} %convolution_bitcast_fusion.1) | copy-start | bytes 786436

commit v2 on v1

--- a/solution.py
+++ b/solution.py
@@ -6,6 +6,7 @@
 from jax import lax
 from jax.experimental import pallas as pl
 from jax.experimental.pallas import tpu as pltpu
+from jax.sharding import Mesh
 from jax.sharding import PartitionSpec as P
 
 HIGHEST = lax.Precision.HIGHEST
@@ -75,7 +76,7 @@
     n_e, spots, used, modes, width,
     first_ref, own_corner, par_corner, own_count,
     re0, re1, im0, im1, pr_ref, pi_ref, own_rec, par_rec, wf_ref, wb_ref, tw_ref,
-    out_ref,
+    out_re, out_im,
     rec, patch_re, patch_im, root, work, acc, light_row, sem,
 ):
     fold = LANES // width
@@ -254,20 +255,22 @@
 
     side = re0.shape[1]
 
+    dests = out_re.shape[0]
+
     def finish(n, carry):
         at = pl.ds(pl.multiple_of(n * SUBS, SUBS), SUBS)
+        dest, far = n % dests, n // dests
         for e in range(n_e):
             for h, (o_re, o_im) in enumerate(((re0, im0), (re1, im1))):
-                cols = slice(h * LANES, (h + 1) * LANES)
                 share = 1.0 / (acc[2, h, e, at, :] + REGULARIZER)
-                out_ref[n, 0, e, :, cols] = o_re[e, at, :] - acc[0, h, e, at, :] * share
-                out_ref[n, 1, e, :, cols] = o_im[e, at, :] - acc[1, h, e, at, :] * share
+                out_re[dest, e, far, h] = o_re[e, at, :] - acc[0, h, e, at, :] * share
+                out_im[dest, e, far, h] = o_im[e, at, :] - acc[1, h, e, at, :] * share
         return carry
 
     lax.fori_loop(0, side // SUBS, finish, 0)
 
 
-def gradient_step(objects, beams, own_rec, par_rec, own_corner, par_corner, own_count, first, n_e, used):
+def gradient_step(objects, beams, own_rec, par_rec, own_corner, par_corner, own_count, first, n_e, used, fars):
     o_re, o_im = objects
     local, side, _ = o_re.shape
     modes, width = beams[0].shape[1], beams[0].shape[-1]
@@ -282,9 +285,10 @@
     whole = pl.BlockSpec(memory_space=pltpu.VMEM)
     rows = used * modes
     n = n_e * used * SUBS
+    out_shape = (side // SUBS // fars, n_e, fars, side // LANES, SUBS, LANES)
     return pl.pallas_call(
         functools.partial(step_kernel, n_e, spots, used, modes, width),
-        out_shape=jax.ShapeDtypeStruct((side // SUBS, 2, n_e, SUBS, side), jnp.float32),
+        out_shape=[jax.ShapeDtypeStruct(out_shape, jnp.float32)] * 2,
         grid_spec=pltpu.PrefetchScalarGridSpec(
             num_scalar_prefetch=4,
             grid=(1,),
@@ -293,9 +297,7 @@
                 pl.BlockSpec(memory_space=pl.ANY), pl.BlockSpec(memory_space=pl.ANY),
                 whole, whole, whole,
             ],
-            out_specs=pl.BlockSpec(
-                (side // SUBS, 2, n_e, SUBS, side), lambda i, *_: (0, 0, 0, 0, 0)
-            ),
+            out_specs=[pl.BlockSpec(out_shape, lambda i, *_: (0,) * len(out_shape))] * 2,
             scratch_shapes=[
                 pltpu.VMEM((n_e, 2 * spots, width, width), jnp.float32),
                 pltpu.VMEM((n, LANES), jnp.float32),
@@ -314,6 +316,101 @@
     )
 
 
+def dot3(a, b):
+    ah, al = split_bf16(a)
+    bh, bl = split_bf16(b)
+    left = jnp.concatenate([ah, al, ah], axis=1)
+    right = jnp.concatenate([bh, bh, bl], axis=0)
+    return jnp.dot(left, right, preferred_element_type=jnp.float32)
+
+
+def project_kernel(fars, halves, project_ref, got_ref, out_ref):
+    energies = project_ref.shape[1]
+    stride = got_ref.shape[0] // energies
+    for f in range(fars):
+        for r in range(SUBS):
+            parts = [
+                got_ref[pl.ds((f * halves + h) * SUBS + r, energies, stride=stride), :]
+                for h in range(halves)
+            ]
+            at = (f * SUBS + r) * halves * LANES
+            values = jnp.concatenate(parts, axis=1)
+            out_ref[:, at:at + halves * LANES] = dot3(project_ref[...], values)
+
+
+def partial_coefs(project, got, fars, halves):
+    rows = got.shape[0]
+    edges, energies = project.shape
+    pixels = rows // energies * LANES
+    return pl.pallas_call(
+        functools.partial(project_kernel, fars, halves),
+        out_shape=jax.ShapeDtypeStruct((edges, pixels), jnp.float32),
+        cost_estimate=pl.CostEstimate(
+            flops=6 * edges * energies * pixels, bytes_accessed=rows * LANES * 4, transcendentals=0
+        ),
+        name="partial_coefs",
+    )(project, got)
+
+
+def fit_kernel(far_ref, mine_ref, theirs_ref, basis_ref, coef_ref, fit_ref):
+    energies = basis_ref.shape[0]
+    own = coef_ref.shape[1]
+    stride = fit_ref.shape[0] // energies
+    at = pl.ds(pl.multiple_of(far_ref[0] * own, own), own)
+    coef_ref[...] = mine_ref[:, at] + theirs_ref[:, at]
+    wide = 2 * LANES
+    for j in range(mine_ref.shape[1] // wide):
+        cols = slice(j * wide, (j + 1) * wide)
+        values = dot3(basis_ref[...], mine_ref[:, cols] + theirs_ref[:, cols])
+        for d in range(energies // SUBS):
+            for u in range(2):
+                to = pl.ds(d * SUBS * stride + j * 2 + u, SUBS, stride=stride)
+                fit_ref[to, :] = values[d * SUBS:(d + 1) * SUBS, u * LANES:(u + 1) * LANES]
+
+
+def fitted_values(far, mine, theirs, basis, own):
+    edges, pixels = mine.shape
+    energies = basis.shape[0]
+    vmem = pl.BlockSpec(memory_space=pltpu.VMEM)
+    return pl.pallas_call(
+        fit_kernel,
+        out_shape=[
+            jax.ShapeDtypeStruct((edges, own), jnp.float32),
+            jax.ShapeDtypeStruct((energies * pixels // LANES, LANES), jnp.float32),
+        ],
+        in_specs=[pl.BlockSpec(memory_space=pltpu.SMEM), vmem, vmem, vmem],
+        out_specs=[vmem, vmem],
+        cost_estimate=pl.CostEstimate(
+            flops=6 * edges * energies * pixels, bytes_accessed=energies * pixels * 4, transcendentals=0
+        ),
+        name="fitted_values",
+    )(far, mine, theirs, basis)
+
+
+def gather_kernel(in_ref, *refs):
+    out_ref = refs[-1]
+    for s in range(in_ref.shape[0]):
+        out_ref[0, :, :, s] = in_ref[s]
+
+
+def gather_part(part, got, out):
+    senders, energies, fars, subs, _ = got.shape
+    step = senders // 2
+    shape = (2, energies, fars, senders, subs, LANES)
+    return pl.pallas_call(
+        gather_kernel,
+        out_shape=jax.ShapeDtypeStruct(shape, jnp.float32),
+        grid=(2,),
+        in_specs=[pl.BlockSpec((step, energies, fars, subs, LANES), lambda i: (i, 0, 0, 0, 0))]
+        + ([] if out is None else [pl.BlockSpec(memory_space=pl.ANY)]),
+        out_specs=pl.BlockSpec(
+            (1, energies, fars, step, subs, LANES), lambda i: (part, 0, 0, i, 0, 0)
+        ),
+        input_output_aliases={} if out is None else {1: 0},
+        name="gather_part",
+    )(*([got] if out is None else [got, out]))
+
+
 def local(
     sample_inphase,
     sample_quadrature,
@@ -327,14 +424,18 @@
     local_energies = sample_inphase.shape[0]
     side = sample_inphase.shape[1]
     spots = recorded_diffraction.shape[2]
-    blocks = lax.axis_size("ea")
+    fars = lax.axis_size("far")
+    cube = lax.axis_size("cube")
+    blocks = fars * cube
     tiles = lax.axis_size("ta")
     tile = lax.axis_index("ta")
     swap = [(0, 1), (1, 0)]
-    assert tiles == 2
+    assert tiles == 2 and fars == 2
     used = spots * 3 // 2
     divided = local_energies % tiles == 0
     n_e = local_energies // tiles if divided else local_energies
+    pix = side * side // (blocks * tiles)
+    two_level = divided and pix == SUBS * side and local_energies == SUBS
     own_rec = recorded_diffraction[:, 0]
     first = tile * n_e if divided else jnp.zeros((), jnp.int32)
     give = lax.dynamic_slice_in_dim(own_rec, (1 - tile) * n_e, n_e, 0) if divided else own_rec
@@ -352,44 +453,63 @@
         first.astype(jnp.int32)[None],
         n_e,
         used,
+        fars if two_level else 1,
     )
     gram = jnp.dot(absorption_templates, absorption_templates.T, precision=HIGHEST)
     factor_low = jnp.linalg.cholesky(gram)
     project = jax.scipy.linalg.cho_solve((factor_low, True), absorption_templates)
-    edges = project.shape[0]
-    pix = side * side // (blocks * tiles)
-    if divided and pix == SUBS * side:
-        got = lax.all_to_all(stepped, ("ea", "ta"), 0, 0, tiled=True)
-        got = got.reshape(blocks * tiles, 2, n_e, pix)
-        values = jnp.moveaxis(got, 1, 0).reshape(2, -1, pix)
+    edges, energies = project.shape
+
+    if two_level:
+        far = lax.axis_index("far")
+        near = energies // fars
+        halves = side // LANES
+        project_near = lax.dynamic_slice_in_dim(project, far * near, near, 1)
+        basis_near = lax.dynamic_slice_in_dim(absorption_templates, far * near, near, 1).T
+        far = far.astype(jnp.int32)[None]
+        out, coefs = None, []
+        got = [lax.all_to_all(x, ("cube", "ta"), 0, 0, tiled=True) for x in stepped]
+        for part in range(2):
+            mine = partial_coefs(project_near, got[part].reshape(-1, LANES), fars, halves)
+            theirs = lax.ppermute(mine, "far", swap)
+            coef, fit = fitted_values(far, mine, theirs, basis_near, pix)
+            coefs.append(coef)
+            back = lax.all_to_all(
+                fit.reshape(cube, local_energies, fars, pix // LANES, LANES), "cube", 0, 0, tiled=True
+            )
+            out = gather_part(part, back, out)
+        return (out.reshape(2, local_energies, blocks, 1, pix), jnp.stack(coefs))
+
+    flat = jnp.stack([x.transpose(1, 0, 2, 4, 3, 5) for x in stepped])
+    if divided:
+        flat = flat.reshape(2, n_e, blocks * tiles, pix)
+        got = lax.all_to_all(flat, ("far", "cube", "ta"), 2, 1, tiled=True)
     else:
-        if divided:
-            parts = blocks * tiles
-            flat = jnp.moveaxis(stepped, 0, 2).reshape(2, n_e, parts, pix)
-            got = lax.all_to_all(flat, ("ea", "ta"), 2, 1, tiled=True)
-        else:
-            flat = jnp.moveaxis(stepped, 0, 2).reshape(2, n_e, blocks, tiles, pix)
-            flat = lax.dynamic_index_in_dim(flat, tile, 3, keepdims=False)
-            got = lax.all_to_all(flat, "ea", 2, 1, tiled=True)
-        values = got.reshape(2, -1, pix)
+        flat = flat.reshape(2, n_e, blocks, tiles, pix)
+        flat = lax.dynamic_index_in_dim(flat, tile, 3, keepdims=False)
+        got = lax.all_to_all(flat, ("far", "cube"), 2, 1, tiled=True)
+    values = got.reshape(2, -1, pix)
     coefs = jnp.einsum("ke,cen->ckn", project, values, precision=HIGHEST)
     fitted_here = jnp.einsum("ke,ckn->cen", absorption_templates, coefs, precision=HIGHEST)
     returned = lax.all_to_all(
-        fitted_here[:, :, None, :], "ea", split_axis=1, concat_axis=2, tiled=True
+        fitted_here[:, :, None, :], ("far", "cube"), split_axis=1, concat_axis=2, tiled=True
     )
     return (returned[:, :, :, None, :], coefs)
 
 
 def solution(mesh):
+    blocks, tiles = mesh.shape["ea"], mesh.shape["ta"]
+    mesh = Mesh(mesh.devices.reshape(2, blocks // 2, tiles), ("far", "cube", "ta"))
+    ea = ("far", "cube")
     in_specs = (
-        P("ea", None, None),
-        P("ea", None, None),
-        P("ea", None, None, None),
-        P("ea", None, None, None),
-        P("ea", "ta", None, None, None),
-        P("ea", "ta", None, None),
-        P("ea", "ta"),
+        P(ea, None, None),
+        P(ea, None, None),
+        P(ea, None, None, None),
+        P(ea, None, None, None),
+        P(ea, "ta", None, None, None),
+        P(ea, "ta", None, None),
+        P(ea, "ta"),
         P(),
     )
-    out_specs = (P(None, "ea", None, "ta", None), P(None, None, ("ea", "ta")))
+    out_specs = (P(None, ea, None, "ta", None), P(None, None, (*ea, "ta")))
     return jax.shard_map(local, mesh=mesh, in_specs=in_specs, out_specs=out_specs, check_vma=False)

time: 156 us -> 128 us (0.82)
  blocking collectives: 53.9 us -> 22.5 us
  Pallas kernels: 19.3 us -> 34.5 us
  starting transfers between devices: 7.84 us -> 22.8 us
  local copies, waits for them, and re-layouts: 19 us -> 8.1 us
  waiting for transfers between devices: 44.5 us -> 33.6 us
  matrix products: 6.43 us -> 0.47 us
    all_to_all x1 -> x3, waiting for transfers between devices: 44.1 us -> 10.4 us  [the longest x2 10.4 us: local(): lax.all_to_all(fit.reshape(cube, local_energies, fars, pix // LANES, LANE...]
    all_to_all x1, blocking collectives: 53.9 us -> 22.5 us  [local(): got = [lax.all_to_all(x, ('cube', 'ta'), 0, 0, tiled=True) for x in stepped]]
    ppermute x0 -> x2, waiting for transfers between devices: none -> 22.8 us  [local(): theirs = lax.ppermute(mine, 'far', swap)]
    pallas_call x0 -> x6, Pallas kernels: none -> 15.1 us  [the longest x2 5.69 us: fitted_values(): pl.pallas_call(fit_kernel, out_shape=[jax.ShapeDtypeStruct((edges, own),...]
    all_to_all x1 -> x3, starting transfers between devices: 7.19 us -> 16.3 us  [the longest x2 12.7 us: local(): lax.all_to_all(fit.reshape(cube, local_energies, fars, pix // LANES, LANE...]
    dot_general x2 -> x0, matrix products: 5.97 us -> none  [the longest x1 4.76 us: local(): jnp.einsum('ke,ckn->cen', absorption_templates, coefs, precision=HIGHEST)]
    ppermute x0 -> x2, starting transfers between devices: none -> 5.87 us  [local(): theirs = lax.ppermute(mine, 'far', swap)]
    reshape x2 -> x0, local copies, waits for them, and re-layouts: 3.94 us -> none  [the longest x1 1.97 us: local(): values = jnp.moveaxis(got, 1, 0).reshape(2, -1, pix)]
  transfers between devices with their start and end apart: 3 -> 7, of which waited for: 2 -> 4; matrix products, arithmetic and copies ran while one was open for 4% -> 7% of each run, Pallas kernels for 0% -> 10%
where the time goes in v2:
time: 128 us; the launch traced here: 127 us
  Pallas kernels  34.5 us (27%)
  waiting for transfers between devices  33.6 us (26%)
  starting transfers between devices  22.8 us (18%)
  blocking collectives  22.5 us (18%)
  local copies, waits for them, and re-layouts  8.1 us (6%)
  other arithmetic  4.75 us (4%)
    ppermute x2, waiting for transfers between devices, local(): theirs = lax.ppermute(mine, 'far', swap)  22.8 us
    all_to_all x1, blocking collectives, local(): got = [lax.all_to_all(x, ('cube', 'ta'), 0, 0, tiled=True) for x in stepped]  22.5 us
    pallas_call x1, Pallas kernels, gradient_step(): pl.pallas_call(functools.partial(step_kernel, n_e, spots, used, modes, wi...  19.4 us
    all_to_all x2, starting transfers between devices, local(): lax.all_to_all(fit.reshape(cube, local_energies, fars, pix // LANES, LANE...  12.7 us
    all_to_all x2, waiting for transfers between devices, local(): lax.all_to_all(fit.reshape(cube, local_energies, fars, pix // LANES, LANE...  10.4 us
    ppermute x2, starting transfers between devices, local(): theirs = lax.ppermute(mine, 'far', swap)  5.87 us
    pallas_call x2, Pallas kernels, fitted_values(): pl.pallas_call(fit_kernel, out_shape=[jax.ShapeDtypeStruct((edges, own),...  5.69 us
    pallas_call x2, Pallas kernels, partial_coefs(): pl.pallas_call(functools.partial(project_kernel, fars, halves), out_shape...  5.32 us
  transfers between devices with their start and end apart: 7, of which 4 were waited for; matrix products, arithmetic and copies ran while one was open for 7% of the time, Pallas kernels for 10%

profile of v2, /device:TPU:0, one launch (start us, length us, event | category | flops | bytes accessed | tf_op | source)
XLA Modules:
  0.0 127.5 jit_solution(3444628822945741004)
XLA Ops:
  0.7 1.4 %dynamic-slice_bitcast_fusion = f32[4,16,32,32]{3,2,1,0:T(8,128)S(1)} fusion(f32[8,1,16,32,32]{4,3,2,1,0:T(8,128)} %param.15, s32[]{:T(128)S(6)} %select_n.13), kind=kLoop, calls=%fused_computation | loop fusion | bytes 524292 | tf_op jit(solution)/shard_map/dynamic_slice | solution.py:441
  2.1 0.6 collective-permute-start.1
  3.0 0.8 reshape.47.pr_ref
  3.8 0.8 reshape.48.pi_ref
  4.9 0.6 copy-done.13
  5.5 0.4 copy-done.4
  5.9 19.4 %gradient_step.1 = (f32[16,4,2,2,8,128]{5,4,3,2,1,0:T(8,128)}, f32[16,4,2,2,8,128]{5,4,3,2,1,0:T(8,128)}) custom-call(s32[1]{0:T(128)} %bitcast.4.first_ref, s32[256]{0:T(256)} %copy-done.12, s32[256]{0:T(256)} %copy-done.13, s32[8]{0:T(128)} %bitcast.47, f32[8,256,256]{2,1,0:T(8,128)} %re1.1, f32[8,256,256]{2,1,0:T(8,128)} %re1.1, f32[8,256,256]{2,1,0:T(8,128)} %im1.1, ...), custom_call_target="tpu_custom_call" | custom-call | tf_op jit(solution)/shard_map/gradient_step/pallas_call | solution.py:289
  25.3 22.5 %all_to_all.20 = f32[16,4,2,2,8,128]{5,4,3,2,1,0:T(8,128)} all-to-all(f32[16,4,2,2,8,128]{5,4,3,2,1,0:T(8,128)} %get-tuple-element.10), channel_id=1, replica_groups=mesh['far'=2,'cube'=8,'ta'=2] {'cube','ta'}, dimensions={0} | all-to-all | bytes 2097152 | tf_op jit(solution)/shard_map/all_to_all | solution.py:471
  47.8 3.7 %all-to-all-start = ((f32[16,4,2,2,8,128]{5,4,3,2,1,0:T(8,128)}), f32[16,4,2,2,8,128]{5,4,3,2,1,0:T(8,128)S(1)}, u32[]{:S(2)}, u32[]{:S(2)}) async-start(f32[16,4,2,2,8,128]{5,4,3,2,1,0:T(8,128)} %get-tuple-element.8), calls=%async_computation | async-start | bytes 2097152 | tf_op jit(solution)/shard_map/all_to_all | solution.py:471
  51.7 1.5 %cholesky.16 = f32[16,16]{1,0:T(8,128)S(1)} custom-call(f32[16,16]{1,0:T(8,128)S(1)} %fusion.5), custom_call_target="Cholesky" | custom-call | tf_op jit(solution)/shard_map/jit(cholesky)/cholesky | solution.py:459
  53.2 0.6 compare_reduce_fusion
  53.8 0.6 fusion
  54.5 1.2 custom-call.10
  56.0 0.7 constant_dynamic-slice_fusion.1.project_ref
  56.7 2.6 %partial_coefs.3.mine_ref = f32[16,4096]{1,0:T(8,128)} custom-call(f32[16,64]{1,0:T(8,128)} %constant_dynamic-slice_fusion.1.project_ref, f32[2048,128]{1,0:T(8,128)} %bitcast.40), custom_call_target="tpu_custom_call" | custom-call | flops 25165824 | bytes 1048576 | tf_op jit(solution)/shard_map/partial_coefs/pallas_call | solution.py:345
  59.4 2.6 %collective-permute-start.3 = (f32[16,4096]{1,0:T(8,128)}, f32[16,4096]{1,0:T(8,128)S(1)}, u32[]{:S(2)}, u32[]{:S(2)}) collective-permute-start(f32[16,4096]{1,0:T(8,128)} %partial_coefs.3.mine_ref), channel_id=1, source_target_pairs={{0,16},{16,0},{1,17},{17,1},{2,18},{18,2},{3,19},{19,3},{4,20},{20... | collective-permute-start | bytes 786440 | tf_op jit(solution)/shard_map/ppermute | solution.py:474
  62.0 0.7 copy.21
  62.7 11.9 %collective-permute-done.3.theirs_ref = f32[16,4096]{1,0:T(8,128)S(1)} collective-permute-done((f32[16,4096]{1,0:T(8,128)}, f32[16,4096]{1,0:T(8,128)S(1)}, u32[]{:S(2)}, u32[]{:S(2)}) %collective-permute-start.3) | collective-permute-done | bytes 262176 | tf_op jit(solution)/shard_map/ppermute | solution.py:474
  74.6 0.7 copy-done.7
  75.3 2.8 %fitted_values.3 = (f32[16,2048]{1,0:T(8,128)}, f32[2048,128]{1,0:T(8,128)}) custom-call(s32[1]{0:T(128)} %bitcast.far_ref, f32[16,4096]{1,0:T(8,128)} %partial_coefs.3.mine_ref, f32[16,4096]{1,0:T(8,128)} %copy-done.7, f32[64,16]{1,0:T(8,128)} %bitcast.43), custom_call_target="tpu_custom_call" | custom-call | flops 25165824 | bytes 1048576 | tf_op jit(solution)/shard_map/fitted_values/pallas_call | solution.py:375
  78.2 4.1 %all-to-all-start.3 = ((f32[8,8,2,16,128]{4,3,2,1,0:T(8,128)}), f32[8,8,2,16,128]{4,3,2,1,0:T(8,128)S(1)}, u32[]{:S(2)}, u32[]{:S(2)}) async-start(f32[8,8,2,16,128]{4,3,2,1,0:T(8,128)} %bitcast.41), calls=%async_computation.3 | async-start | bytes 2097152 | tf_op jit(solution)/shard_map/all_to_all | solution.py:477
  82.3 2.7 %partial_coefs.2.mine_ref = f32[16,4096]{1,0:T(8,128)} custom-call(f32[16,64]{1,0:T(8,128)} %constant_dynamic-slice_fusion.1.project_ref, f32[2048,128]{1,0:T(8,128)} %bitcast.39), custom_call_target="tpu_custom_call" | custom-call | flops 25165824 | bytes 1048576 | tf_op jit(solution)/shard_map/partial_coefs/pallas_call | solution.py:345
  84.9 3.3 %collective-permute-start.2 = (f32[16,4096]{1,0:T(8,128)}, f32[16,4096]{1,0:T(8,128)S(1)}, u32[]{:S(2)}, u32[]{:S(2)}) collective-permute-start(f32[16,4096]{1,0:T(8,128)} %partial_coefs.2.mine_ref), channel_id=1, source_target_pairs={{0,16},{16,0},{1,17},{17,1},{2,18},{18,2},{3,19},{19,3},{4,20},{20... | collective-permute-start | bytes 786440 | tf_op jit(solution)/shard_map/ppermute | solution.py:474
  88.2 10.9 %collective-permute-done.2.theirs_ref = f32[16,4096]{1,0:T(8,128)S(1)} collective-permute-done((f32[16,4096]{1,0:T(8,128)}, f32[16,4096]{1,0:T(8,128)S(1)}, u32[]{:S(2)}, u32[]{:S(2)}) %collective-permute-start.2) | collective-permute-done | bytes 262176 | tf_op jit(solution)/shard_map/ppermute | solution.py:474
  99.1 0.7 copy-done.8
  99.8 2.9 %fitted_values.2 = (f32[16,2048]{1,0:T(8,128)}, f32[2048,128]{1,0:T(8,128)}) custom-call(s32[1]{0:T(128)} %bitcast.far_ref, f32[16,4096]{1,0:T(8,128)} %partial_coefs.2.mine_ref, f32[16,4096]{1,0:T(8,128)} %copy-done.8, f32[64,16]{1,0:T(8,128)} %bitcast.44), custom_call_target="tpu_custom_call" | custom-call | flops 25165824 | bytes 1048576 | tf_op jit(solution)/shard_map/fitted_values/pallas_call | solution.py:375
  102.6 8.6 %all-to-all-start.1 = ((f32[8,8,2,16,128]{4,3,2,1,0:T(8,128)}), f32[8,8,2,16,128]{4,3,2,1,0:T(8,128)S(1)}, u32[]{:S(2)}, u32[]{:S(2)}) async-start(f32[8,8,2,16,128]{4,3,2,1,0:T(8,128)} %bitcast.42), calls=%async_computation.1 | async-start | bytes 2097152 | tf_op jit(solution)/shard_map/all_to_all | solution.py:477
  111.2 0.7 pad_maximum_fusion
  112.0 2.0 %gather_part.2.refs_0_ = f32[2,8,2,8,16,128]{5,4,3,2,1,0:T(8,128)} custom-call(f32[8,8,2,16,128]{4,3,2,1,0:T(8,128)} %copy-done.1), custom_call_target="tpu_custom_call" | custom-call | tf_op jit(solution)/shard_map/gather_part/pallas_call | solution.py:400
  114.0 10.4 %all-to-all-done.1.in_ref = f32[8,8,2,16,128]{4,3,2,1,0:T(8,128)S(1)} async-done(((f32[8,8,2,16,128]{4,3,2,1,0:T(8,128)}), f32[8,8,2,16,128]{4,3,2,1,0:T(8,128)S(1)}, u32[]{:S(2)}, u32[]{:S(2)}) %all-to-all-start.1) | async-done | bytes 1048608 | tf_op jit(solution)/shard_map/all_to_all | solution.py:477
  124.4 1.0 copy-done.2
  125.4 2.0 %gather_part.3 = f32[2,8,2,8,16,128]{5,4,3,2,1,0:T(8,128)} custom-call(f32[8,8,2,16,128]{4,3,2,1,0:T(8,128)} %copy-done.2, f32[2,8,2,8,16,128]{5,4,3,2,1,0:T(8,128)} %gather_part.2.refs_0_), custom_call_target="tpu_custom_call", output_to_operand_aliasing={{}: (1, {})} | custom-call | tf_op jit(solution)/shard_map/gather_part/pallas_call | solution.py:400
  (37 shorter events, 1.4 us)
Async XLA Ops:
  0.6 50.8 %copy-start = (f32[16,128]{1,0:T(8,128)S(1)}, f32[16,128]{1,0:T(8,128)}, u32[]{:S(2)}) copy-start(f32[16,128]{1,0:T(8,128)} %param.18) | copy-start | bytes 24580
  0.6 2.0 %copy-start.11 = (s32[8,1,16,2]{2,3,1,0:T(2,128)S(1)}, s32[8,1,16,2]{2,3,1,0:T(2,128)}, u32[]{:S(2)}) copy-start(s32[8,1,16,2]{2,3,1,0:T(2,128)} %param.16) | copy-start | bytes 3076
  0.7 2.3 %copy-start.5 = (f32[8,3,32,32]{3,2,1,0:T(8,128)S(1)}, f32[8,3,32,32]{3,2,1,0:T(8,128)}, u32[]{:S(2)}) copy-start(f32[8,3,32,32]{3,2,1,0:T(8,128)} %param.13) | copy-start | bytes 294916
  0.7 3.1 %copy-start.6 = (f32[8,3,32,32]{3,2,1,0:T(8,128)S(1)}, f32[8,3,32,32]{3,2,1,0:T(8,128)}, u32[]{:S(2)}) copy-start(f32[8,3,32,32]{3,2,1,0:T(8,128)} %param.14) | copy-start | bytes 294916
  2.1 2.9 %collective-permute-start.1 = (f32[4,16,32,32]{3,2,1,0:T(8,128)S(1)}, f32[4,16,32,32]{3,2,1,0:T(8,128)S(1)}, u32[]{:S(2)}, u32[]{:S(2)}) collective-permute-start(f32[4,16,32,32]{3,2,1,0:T(8,128)S(1)} %dynamic-slice_bitcast_fusion), channel_id=1, source_target_pairs={{0,1},{1,0},{2,3},{3,2},{4,5},{5,4},{6,7},{7,6},{8,9},{9,8},{10,11... | collective-permute-start | bytes 786440 | tf_op jit(solution)/shard_map/ppermute | solution.py:442
  2.9 2.0 %copy-start.12 = (s32[256]{0:T(256)}, s32[256]{0:T(256)S(1)}, u32[]{:S(2)}) copy-start(s32[256]{0:T(256)S(1)} %reshape.45.own_corner) | copy-start | bytes 3076
  2.9 2.0 %collective-permute-start = (s32[256]{0:T(256)S(1)}, s32[256]{0:T(256)S(1)}, u32[]{:S(2)}, u32[]{:S(2)}) collective-permute-start(s32[256]{0:T(256)S(1)} %reshape.45.own_corner), channel_id=1, source_target_pairs={{0,1},{1,0},{2,3},{3,2},{4,5},{5,4},{6,7},{7,6},{8,9},{9,8},{10,11... | collective-permute-start | bytes 3080 | tf_op jit(solution)/shard_map/ppermute | solution.py:444
  4.9 0.6 copy-start.13
  4.9 1.0 copy-start.4
  47.8 30.4 %all-to-all-start = ((f32[16,4,2,2,8,128]{5,4,3,2,1,0:T(8,128)}), f32[16,4,2,2,8,128]{5,4,3,2,1,0:T(8,128)S(1)}, u32[]{:S(2)}, u32[]{:S(2)}) async-start(f32[16,4,2,2,8,128]{5,4,3,2,1,0:T(8,128)} %get-tuple-element.8), calls=%async_computation | async-start | bytes 2097152 | tf_op jit(solution)/shard_map/all_to_all | solution.py:471
  59.4 15.3 %collective-permute-start.3 = (f32[16,4096]{1,0:T(8,128)}, f32[16,4096]{1,0:T(8,128)S(1)}, u32[]{:S(2)}, u32[]{:S(2)}) collective-permute-start(f32[16,4096]{1,0:T(8,128)} %partial_coefs.3.mine_ref), channel_id=1, source_target_pairs={{0,16},{16,0},{1,17},{17,1},{2,18},{18,2},{3,19},{19,3},{4,20},{20... | collective-permute-start | bytes 786440 | tf_op jit(solution)/shard_map/ppermute | solution.py:474
  74.6 0.7 copy-start.7
  78.2 4.1 %copy-start.3 = (f32[16,4,2,2,8,128]{5,4,3,2,1,0:T(8,128)}, f32[16,4,2,2,8,128]{5,4,3,2,1,0:T(8,128)S(1)}, u32[]{:S(2)}) copy-start(f32[16,4,2,2,8,128]{5,4,3,2,1,0:T(8,128)S(1)} %all-to-all-done) | copy-start | bytes 3145732
  78.2 24.5 %all-to-all-start.3 = ((f32[8,8,2,16,128]{4,3,2,1,0:T(8,128)}), f32[8,8,2,16,128]{4,3,2,1,0:T(8,128)S(1)}, u32[]{:S(2)}, u32[]{:S(2)}) async-start(f32[8,8,2,16,128]{4,3,2,1,0:T(8,128)} %bitcast.41), calls=%async_computation.3 | async-start | bytes 2097152 | tf_op jit(solution)/shard_map/all_to_all | solution.py:477
  82.3 29.0 %copy-start.9 = (f32[16,2048]{1,0:T(8,128)S(1)}, f32[16,2048]{1,0:T(8,128)}, u32[]{:S(2)}) copy-start(f32[16,2048]{1,0:T(8,128)} %get-tuple-element.12) | copy-start | bytes 393220
  84.9 14.1 %collective-permute-start.2 = (f32[16,4096]{1,0:T(8,128)}, f32[16,4096]{1,0:T(8,128)S(1)}, u32[]{:S(2)}, u32[]{:S(2)}) collective-permute-start(f32[16,4096]{1,0:T(8,128)} %partial_coefs.2.mine_ref), channel_id=1, source_target_pairs={{0,16},{16,0},{1,17},{17,1},{2,18},{18,2},{3,19},{19,3},{4,20},{20... | collective-permute-start | bytes 786440 | tf_op jit(solution)/shard_map/ppermute | solution.py:474
  99.1 0.7 copy-start.8
  102.6 8.6 %copy-start.10 = (f32[16,2048]{1,0:T(8,128)S(1)}, f32[16,2048]{1,0:T(8,128)}, u32[]{:S(2)}) copy-start(f32[16,2048]{1,0:T(8,128)} %get-tuple-element.13) | copy-start | bytes 393220
  102.6 9.3 %copy-start.1 = (f32[8,8,2,16,128]{4,3,2,1,0:T(8,128)}, f32[8,8,2,16,128]{4,3,2,1,0:T(8,128)S(1)}, u32[]{:S(2)}) copy-start(f32[8,8,2,16,128]{4,3,2,1,0:T(8,128)S(1)} %all-to-all-done.3.in_ref) | copy-start | bytes 3145732
  102.6 21.8 %all-to-all-start.1 = ((f32[8,8,2,16,128]{4,3,2,1,0:T(8,128)}), f32[8,8,2,16,128]{4,3,2,1,0:T(8,128)S(1)}, u32[]{:S(2)}, u32[]{:S(2)}) async-start(f32[8,8,2,16,128]{4,3,2,1,0:T(8,128)} %bitcast.42), calls=%async_computation.1 | async-start | bytes 2097152 | tf_op jit(solution)/shard_map/all_to_all | solution.py:477
  124.4 1.0 copy-start.2

commit v3 on v2

--- a/solution.py
+++ b/solution.py
@@ -14,6 +14,7 @@
 REGULARIZER = 1.0
 LANES = 128
 SUBS = 8
+SMALL = 12 << 20
 
 
 def split_bf16(x):
@@ -348,6 +349,7 @@
         cost_estimate=pl.CostEstimate(
             flops=6 * edges * energies * pixels, bytes_accessed=rows * LANES * 4, transcendentals=0
         ),
+        compiler_params=pltpu.CompilerParams(vmem_limit_bytes=SMALL),
         name="partial_coefs",
     )(project, got)
 
@@ -383,30 +385,35 @@
         cost_estimate=pl.CostEstimate(
             flops=6 * edges * energies * pixels, bytes_accessed=energies * pixels * 4, transcendentals=0
         ),
+        compiler_params=pltpu.CompilerParams(vmem_limit_bytes=SMALL),
         name="fitted_values",
     )(far, mine, theirs, basis)
 
 
-def gather_kernel(in_ref, *refs):
-    out_ref = refs[-1]
-    for s in range(in_ref.shape[0]):
-        out_ref[0, :, :, s] = in_ref[s]
+def gather_kernel(part, in_ref, *refs):
+    out_ref, sem = refs[-2:]
+    copies = [
+        pltpu.make_async_copy(in_ref.at[s], out_ref.at[part, :, :, s], sem.at[s])
+        for s in range(in_ref.shape[0])
+    ]
+    for c in copies:
+        c.start()
+    for c in copies:
+        c.wait()
 
 
 def gather_part(part, got, out):
     senders, energies, fars, subs, _ = got.shape
-    step = senders // 2
     shape = (2, energies, fars, senders, subs, LANES)
+    hbm = pl.BlockSpec(memory_space=pl.ANY)
     return pl.pallas_call(
-        gather_kernel,
+        functools.partial(gather_kernel, part),
         out_shape=jax.ShapeDtypeStruct(shape, jnp.float32),
-        grid=(2,),
-        in_specs=[pl.BlockSpec((step, energies, fars, subs, LANES), lambda i: (i, 0, 0, 0, 0))]
-        + ([] if out is None else [pl.BlockSpec(memory_space=pl.ANY)]),
-        out_specs=pl.BlockSpec(
-            (1, energies, fars, step, subs, LANES), lambda i: (part, 0, 0, i, 0, 0)
-        ),
+        in_specs=[pl.BlockSpec(memory_space=pltpu.VMEM)] + ([] if out is None else [hbm]),
+        out_specs=hbm,
+        scratch_shapes=[pltpu.SemaphoreType.DMA((senders,))],
         input_output_aliases={} if out is None else {1: 0},
+        compiler_params=pltpu.CompilerParams(vmem_limit_bytes=SMALL),
         name="gather_part",
     )(*([got] if out is None else [got, out]))
 
@@ -468,7 +475,10 @@
         basis_near = lax.dynamic_slice_in_dim(absorption_templates, far * near, near, 1).T
         far = far.astype(jnp.int32)[None]
         out, coefs = None, []
-        got = [lax.all_to_all(x, ("cube", "ta"), 0, 0, tiled=True) for x in stepped]
+        later, project_near, basis_near = lax.optimization_barrier(
+            (stepped[1], project_near, basis_near)
+        )
+        got = [lax.all_to_all(x, ("cube", "ta"), 0, 0, tiled=True) for x in (stepped[0], later)]
         for part in range(2):
             mine = partial_coefs(project_near, got[part].reshape(-1, LANES), fars, halves)
             theirs = lax.ppermute(mine, "far", swap)

time: 128 us -> 118 us (0.922)
  waiting for transfers between devices: 33.6 us -> 57.1 us
  blocking collectives: 22.5 us -> 0 us
  Pallas kernels: 34.5 us -> 26.5 us
  local copies, waits for them, and re-layouts: 8.1 us -> 4.49 us
    all_to_all x1 -> x0, blocking collectives: 22.5 us -> none  [local(): got = [lax.all_to_all(x, ('cube', 'ta'), 0, 0, tiled=True) for x in stepped]]
    all_to_all x1 -> x2, waiting for transfers between devices: 0.01 us -> 13.5 us  [local(): lax.all_to_all(x, ('cube', 'ta'), 0, 0, tiled=True)]
    ppermute x2, waiting for transfers between devices: 22.8 us -> 30.5 us  [local(): theirs = lax.ppermute(mine, 'far', swap)]
    all_to_all x1 -> x2, starting transfers between devices: 3.65 us -> 9.86 us  [local(): lax.all_to_all(x, ('cube', 'ta'), 0, 0, tiled=True)]
    pallas_call x2, Pallas kernels: 5.32 us -> 1.37 us  [partial_coefs(): pl.pallas_call(functools.partial(project_kernel, fars, halves), out_shape...]
    ppermute x2, starting transfers between devices: 5.87 us -> 2.6 us  [local(): theirs = lax.ppermute(mine, 'far', swap)]
    unnamed x30 -> x16, local copies, waits for them, and re-layouts: 4.21 us -> 1.2 us
    all_to_all x2, starting transfers between devices: 12.7 us -> 10 us  [local(): lax.all_to_all(fit.reshape(cube, local_energies, fars, pix // LANES, LANE...]
  transfers between devices with their start and end apart: 7 -> 8, of which waited for: 4 -> 7; matrix products, arithmetic and copies ran while one was open for 7% -> 6% of each run, Pallas kernels for 10% -> 5%
where the time goes in v3:
time: 118 us; the launch traced here: 117 us
  waiting for transfers between devices  57.1 us (48%)
  Pallas kernels  26.5 us (22%)
  starting transfers between devices  23.1 us (20%)
  other arithmetic  4.74 us (4%)
  local copies, waits for them, and re-layouts  4.49 us (4%)
    ppermute x2, waiting for transfers between devices, local(): theirs = lax.ppermute(mine, 'far', swap)  30.5 us
    pallas_call x1, Pallas kernels, gradient_step(): pl.pallas_call(functools.partial(step_kernel, n_e, spots, used, modes, wi...  19.5 us
    all_to_all x2, waiting for transfers between devices, local(): lax.all_to_all(x, ('cube', 'ta'), 0, 0, tiled=True)  13.5 us
    all_to_all x2, waiting for transfers between devices, local(): lax.all_to_all(fit.reshape(cube, local_energies, fars, pix // LANES, LANE...  12.7 us
    all_to_all x2, starting transfers between devices, local(): lax.all_to_all(fit.reshape(cube, local_energies, fars, pix // LANES, LANE...  10 us
    all_to_all x2, starting transfers between devices, local(): lax.all_to_all(x, ('cube', 'ta'), 0, 0, tiled=True)  9.86 us
    pallas_call x2, Pallas kernels, fitted_values(): pl.pallas_call(fit_kernel, out_shape=[jax.ShapeDtypeStruct((edges, own),...  3.58 us
    ppermute x2, starting transfers between devices, local(): theirs = lax.ppermute(mine, 'far', swap)  2.6 us
  transfers between devices with their start and end apart: 8, of which 7 were waited for; matrix products, arithmetic and copies ran while one was open for 6% of the time, Pallas kernels for 5%

profile of v3, /device:TPU:0, one launch (start us, length us, event | category | flops | bytes accessed | tf_op | source)
XLA Modules:
  0.0 117.1 jit_solution(1810179246895814644)
XLA Ops:
  0.7 1.4 %dynamic-slice_bitcast_fusion = f32[4,16,32,32]{3,2,1,0:T(8,128)S(1)} fusion(f32[8,1,16,32,32]{4,3,2,1,0:T(8,128)} %param.15, s32[]{:T(128)S(6)} %select_n.11), kind=kLoop, calls=%fused_computation | loop fusion | bytes 524292 | tf_op jit(solution)/shard_map/dynamic_slice | solution.py:448
  2.1 0.6 collective-permute-start.1
  3.0 0.8 reshape.47.pr_ref
  3.8 0.8 reshape.48.pi_ref
  4.5 0.4 collective-permute-done.par_corner
  4.9 0.6 copy-done.6
  5.5 0.4 copy-done.1
  5.9 19.5 %gradient_step.1 = (f32[16,4,2,2,8,128]{5,4,3,2,1,0:T(8,128)}, f32[16,4,2,2,8,128]{5,4,3,2,1,0:T(8,128)}) custom-call(s32[1]{0:T(128)} %bitcast.1.first_ref, s32[256]{0:T(256)} %copy-done.5, s32[256]{0:T(256)} %copy-done.6, s32[8]{0:T(128)} %bitcast.45, f32[8,256,256]{2,1,0:T(8,128)} %re1.1, f32[8,256,256]{2,1,0:T(8,128)} %re1.1, f32[8,256,256]{2,1,0:T(8,128)} %im1.1, ...), custom_call_target="tpu_custom_call" | custom-call | tf_op jit(solution)/shard_map/gradient_step/pallas_call | solution.py:290
  25.3 6.2 %all-to-all-start.2 = ((f32[16,4,2,2,8,128]{5,4,3,2,1,0:T(8,128)}), f32[16,4,2,2,8,128]{5,4,3,2,1,0:T(8,128)S(1)}, u32[]{:S(2)}, u32[]{:S(2)}) async-start(f32[16,4,2,2,8,128]{5,4,3,2,1,0:T(8,128)} %get-tuple-element.16), calls=%async_computation.2 | async-start | bytes 2097152 | tf_op jit(solution)/shard_map/all_to_all | solution.py:481
  31.8 1.5 %cholesky.16 = f32[16,16]{1,0:T(8,128)S(1)} custom-call(f32[16,16]{1,0:T(8,128)S(1)} %fusion.5), custom_call_target="Cholesky" | custom-call | tf_op jit(solution)/shard_map/jit(cholesky)/cholesky | solution.py:466
  33.3 0.6 compare_reduce_fusion
  33.9 0.6 fusion
  34.6 1.2 %custom-call.10 = f32[1,16,16]{1,2,0:T(8,128)S(1)} custom-call(f32[1,16,16]{2,1,0:T(8,128)S(1)} %fusion), custom_call_target="InvertDiagBlocksLowerTriangular" | custom-call | tf_op jit(solution)/shard_map/jit(_cho_solve)/triangular_solve | solution.py:467
  36.0 0.2 fusion.3
  36.2 0.1 fusion.1
  36.4 11.3 %all-to-all-done.2 = f32[16,4,2,2,8,128]{5,4,3,2,1,0:T(8,128)S(1)} async-done(((f32[16,4,2,2,8,128]{5,4,3,2,1,0:T(8,128)}), f32[16,4,2,2,8,128]{5,4,3,2,1,0:T(8,128)S(1)}, u32[]{:S(2)}, u32[]{:S(2)}) %all-to-all-start.2) | async-done | bytes 1048608 | tf_op jit(solution)/shard_map/all_to_all | solution.py:481
  47.7 3.7 %all-to-all-start = ((f32[16,4,2,2,8,128]{5,4,3,2,1,0:T(8,128)}), f32[16,4,2,2,8,128]{5,4,3,2,1,0:T(8,128)S(1)}, u32[]{:S(2)}, u32[]{:S(2)}) async-start(f32[16,4,2,2,8,128]{5,4,3,2,1,0:T(8,128)} %get-tuple-element.13), calls=%async_computation | async-start | bytes 2097152 | tf_op jit(solution)/shard_map/all_to_all | solution.py:481
  51.3 0.7 partial_coefs.3.mine_ref
  52.0 2.6 %collective-permute-start.3 = (f32[16,4096]{1,0:T(8,128)S(1)}, f32[16,4096]{1,0:T(8,128)S(1)}, u32[]{:S(2)}, u32[]{:S(2)}) collective-permute-start(f32[16,4096]{1,0:T(8,128)S(1)} %partial_coefs.3.mine_ref), channel_id=1, source_target_pairs={{0,16},{16,0},{1,17},{17,1},{2,18},{18,2},{3,19},{19,3},{4,20},{20... | collective-permute-start | bytes 786440 | tf_op jit(solution)/shard_map/ppermute | solution.py:484
  54.6 14.5 %collective-permute-done.3.theirs_ref = f32[16,4096]{1,0:T(8,128)S(1)} collective-permute-done((f32[16,4096]{1,0:T(8,128)S(1)}, f32[16,4096]{1,0:T(8,128)S(1)}, u32[]{:S(2)}, u32[]{:S(2)}) %collective-permute-start.3) | collective-permute-done | bytes 262176 | tf_op jit(solution)/shard_map/ppermute | solution.py:484
  69.1 1.8 %fitted_values.3 = (f32[16,2048]{1,0:T(8,128)S(1)}, f32[2048,128]{1,0:T(8,128)}) custom-call(s32[1]{0:T(128)} %bitcast.far_ref, f32[16,4096]{1,0:T(8,128)S(1)} %partial_coefs.3.mine_ref, f32[16,4096]{1,0:T(8,128)S(1)} %collective-permute-done.3.theirs_ref, f32[64,16]{1,0:T(8,128)S(1)} %bitcast.39), custom_call_target="tpu_custom_call" | custom-call | flops 25165824 | bytes 1048576 | tf_op jit(solution)/shard_map/fitted_values/pallas_call | solution.py:377
  70.9 2.2 %all-to-all-done = f32[16,4,2,2,8,128]{5,4,3,2,1,0:T(8,128)S(1)} async-done(((f32[16,4,2,2,8,128]{5,4,3,2,1,0:T(8,128)}), f32[16,4,2,2,8,128]{5,4,3,2,1,0:T(8,128)S(1)}, u32[]{:S(2)}, u32[]{:S(2)}) %all-to-all-start) | async-done | bytes 1048608 | tf_op jit(solution)/shard_map/all_to_all | solution.py:481
  73.1 5.7 %all-to-all-start.3 = ((f32[8,8,2,16,128]{4,3,2,1,0:T(8,128)}), f32[8,8,2,16,128]{4,3,2,1,0:T(8,128)S(1)}, u32[]{:S(2)}, u32[]{:S(2)}) async-start(f32[8,8,2,16,128]{4,3,2,1,0:T(8,128)} %bitcast.12), calls=%async_computation.3 | async-start | bytes 2097152 | tf_op jit(solution)/shard_map/all_to_all | solution.py:487
  78.7 0.7 partial_coefs.2.mine_ref
  79.4 16.0 %collective-permute-done.2.theirs_ref = f32[16,4096]{1,0:T(8,128)S(1)} collective-permute-done((f32[16,4096]{1,0:T(8,128)S(1)}, f32[16,4096]{1,0:T(8,128)S(1)}, u32[]{:S(2)}, u32[]{:S(2)}) %collective-permute-start.2) | collective-permute-done | bytes 262176 | tf_op jit(solution)/shard_map/ppermute | solution.py:484
  95.4 1.8 %fitted_values.2 = (f32[16,2048]{1,0:T(8,128)S(1)}, f32[2048,128]{1,0:T(8,128)}) custom-call(s32[1]{0:T(128)} %bitcast.far_ref, f32[16,4096]{1,0:T(8,128)S(1)} %partial_coefs.2.mine_ref, f32[16,4096]{1,0:T(8,128)S(1)} %collective-permute-done.2.theirs_ref, f32[64,16]{1,0:T(8,128)S(1)} %bitcast.40), custom_call_target="tpu_custom_call" | custom-call | flops 25165824 | bytes 1048576 | tf_op jit(solution)/shard_map/fitted_values/pallas_call | solution.py:377
  97.2 0.8 all-to-all-done.3.in_ref
  98.1 4.3 %all-to-all-start.1 = ((f32[8,8,2,16,128]{4,3,2,1,0:T(8,128)}), f32[8,8,2,16,128]{4,3,2,1,0:T(8,128)S(1)}, u32[]{:S(2)}, u32[]{:S(2)}) async-start(f32[8,8,2,16,128]{4,3,2,1,0:T(8,128)} %bitcast.10), calls=%async_computation.1 | async-start | bytes 2097152 | tf_op jit(solution)/shard_map/all_to_all | solution.py:487
  102.4 0.7 pad_maximum_fusion
  103.1 1.0 gather_part.2.refs_0_
  104.2 11.9 %all-to-all-done.1.in_ref = f32[8,8,2,16,128]{4,3,2,1,0:T(8,128)S(1)} async-done(((f32[8,8,2,16,128]{4,3,2,1,0:T(8,128)}), f32[8,8,2,16,128]{4,3,2,1,0:T(8,128)S(1)}, u32[]{:S(2)}, u32[]{:S(2)}) %all-to-all-start.1) | async-done | bytes 1048608 | tf_op jit(solution)/shard_map/all_to_all | solution.py:487
  116.1 1.0 gather_part.3
  (24 shorter events, 0.9 us)
Async XLA Ops:
  0.6 30.9 %copy-start = (f32[16,128]{1,0:T(8,128)S(1)}, f32[16,128]{1,0:T(8,128)}, u32[]{:S(2)}) copy-start(f32[16,128]{1,0:T(8,128)} %param.18) | copy-start | bytes 24580
  0.6 2.0 %copy-start.4 = (s32[8,1,16,2]{2,3,1,0:T(2,128)S(1)}, s32[8,1,16,2]{2,3,1,0:T(2,128)}, u32[]{:S(2)}) copy-start(s32[8,1,16,2]{2,3,1,0:T(2,128)} %param.16) | copy-start | bytes 3076
  0.7 2.3 %copy-start.2 = (f32[8,3,32,32]{3,2,1,0:T(8,128)S(1)}, f32[8,3,32,32]{3,2,1,0:T(8,128)}, u32[]{:S(2)}) copy-start(f32[8,3,32,32]{3,2,1,0:T(8,128)} %param.13) | copy-start | bytes 294916
  0.7 3.1 %copy-start.3 = (f32[8,3,32,32]{3,2,1,0:T(8,128)S(1)}, f32[8,3,32,32]{3,2,1,0:T(8,128)}, u32[]{:S(2)}) copy-start(f32[8,3,32,32]{3,2,1,0:T(8,128)} %param.14) | copy-start | bytes 294916
  2.1 2.9 %collective-permute-start.1 = (f32[4,16,32,32]{3,2,1,0:T(8,128)S(1)}, f32[4,16,32,32]{3,2,1,0:T(8,128)S(1)}, u32[]{:S(2)}, u32[]{:S(2)}) collective-permute-start(f32[4,16,32,32]{3,2,1,0:T(8,128)S(1)} %dynamic-slice_bitcast_fusion), channel_id=1, source_target_pairs={{0,1},{1,0},{2,3},{3,2},{4,5},{5,4},{6,7},{7,6},{8,9},{9,8},{10,11... | collective-permute-start | bytes 786440 | tf_op jit(solution)/shard_map/ppermute | solution.py:449
  2.9 2.0 %copy-start.5 = (s32[256]{0:T(256)}, s32[256]{0:T(256)S(1)}, u32[]{:S(2)}) copy-start(s32[256]{0:T(256)S(1)} %reshape.45.own_corner) | copy-start | bytes 3076
  2.9 2.0 %collective-permute-start = (s32[256]{0:T(256)S(1)}, s32[256]{0:T(256)S(1)}, u32[]{:S(2)}, u32[]{:S(2)}) collective-permute-start(s32[256]{0:T(256)S(1)} %reshape.45.own_corner), channel_id=1, source_target_pairs={{0,1},{1,0},{2,3},{3,2},{4,5},{5,4},{6,7},{7,6},{8,9},{9,8},{10,11... | collective-permute-start | bytes 3080 | tf_op jit(solution)/shard_map/ppermute | solution.py:451
  4.9 0.6 copy-start.6
  4.9 1.0 copy-start.1
  25.3 22.3 %all-to-all-start.2 = ((f32[16,4,2,2,8,128]{5,4,3,2,1,0:T(8,128)}), f32[16,4,2,2,8,128]{5,4,3,2,1,0:T(8,128)S(1)}, u32[]{:S(2)}, u32[]{:S(2)}) async-start(f32[16,4,2,2,8,128]{5,4,3,2,1,0:T(8,128)} %get-tuple-element.16), calls=%async_computation.2 | async-start | bytes 2097152 | tf_op jit(solution)/shard_map/all_to_all | solution.py:481
  47.7 25.4 %all-to-all-start = ((f32[16,4,2,2,8,128]{5,4,3,2,1,0:T(8,128)}), f32[16,4,2,2,8,128]{5,4,3,2,1,0:T(8,128)S(1)}, u32[]{:S(2)}, u32[]{:S(2)}) async-start(f32[16,4,2,2,8,128]{5,4,3,2,1,0:T(8,128)} %get-tuple-element.13), calls=%async_computation | async-start | bytes 2097152 | tf_op jit(solution)/shard_map/all_to_all | solution.py:481
  52.0 17.1 %collective-permute-start.3 = (f32[16,4096]{1,0:T(8,128)S(1)}, f32[16,4096]{1,0:T(8,128)S(1)}, u32[]{:S(2)}, u32[]{:S(2)}) collective-permute-start(f32[16,4096]{1,0:T(8,128)S(1)} %partial_coefs.3.mine_ref), channel_id=1, source_target_pairs={{0,16},{16,0},{1,17},{17,1},{2,18},{18,2},{3,19},{19,3},{4,20},{20... | collective-permute-start | bytes 786440 | tf_op jit(solution)/shard_map/ppermute | solution.py:484
  73.1 25.0 %all-to-all-start.3 = ((f32[8,8,2,16,128]{4,3,2,1,0:T(8,128)}), f32[8,8,2,16,128]{4,3,2,1,0:T(8,128)S(1)}, u32[]{:S(2)}, u32[]{:S(2)}) async-start(f32[8,8,2,16,128]{4,3,2,1,0:T(8,128)} %bitcast.12), calls=%async_computation.3 | async-start | bytes 2097152 | tf_op jit(solution)/shard_map/all_to_all | solution.py:487
  79.4 16.0 %collective-permute-start.2 = (f32[16,4096]{1,0:T(8,128)S(1)}, f32[16,4096]{1,0:T(8,128)S(1)}, u32[]{:S(2)}, u32[]{:S(2)}) collective-permute-start(f32[16,4096]{1,0:T(8,128)S(1)} %partial_coefs.2.mine_ref), channel_id=1, source_target_pairs={{0,16},{16,0},{1,17},{17,1},{2,18},{18,2},{3,19},{19,3},{4,20},{20... | collective-permute-start | bytes 786440 | tf_op jit(solution)/shard_map/ppermute | solution.py:484
  98.1 18.0 %all-to-all-start.1 = ((f32[8,8,2,16,128]{4,3,2,1,0:T(8,128)}), f32[8,8,2,16,128]{4,3,2,1,0:T(8,128)S(1)}, u32[]{:S(2)}, u32[]{:S(2)}) async-start(f32[8,8,2,16,128]{4,3,2,1,0:T(8,128)} %bitcast.10), calls=%async_computation.1 | async-start | bytes 2097152 | tf_op jit(solution)/shard_map/all_to_all | solution.py:487

commit v4 on v3

--- a/solution.py
+++ b/solution.py
@@ -15,6 +15,7 @@
 LANES = 128
 SUBS = 8
 SMALL = 12 << 20
+LARGE = 60 << 20
 
 
 def split_bf16(x):
@@ -75,35 +76,64 @@
 
 def step_kernel(
     n_e, spots, used, modes, width,
-    first_ref, own_corner, par_corner, own_count,
-    re0, re1, im0, im1, pr_ref, pi_ref, own_rec, par_rec, wf_ref, wb_ref, tw_ref,
+    first_ref, table_ref,
+    o_re, o_im, pr_hbm, pi_hbm, own_rec, par_rec, wf_hbm, wb_hbm, tw_hbm,
     out_re, out_im,
-    rec, patch_re, patch_im, root, work, acc, light_row, sem,
+    obj, rec, pr_ref, pi_ref, wf_ref, wb_ref, tw_ref, patch, term, root, work, acc, stage,
+    obj_sem, rec_sem, shared_sem, out_sem,
 ):
     fold = LANES // width
     groups = used // SUBS
     per_group = modes * SUBS
-    rows = groups * per_group
+    per_q = groups * per_group
+    side = obj.shape[3]
     first = first_ref[0]
-    copies = [
-        pltpu.make_async_copy(own_rec.at[pl.ds(first, n_e)], rec.at[:, pl.ds(0, spots)], sem.at[0]),
-        pltpu.make_async_copy(par_rec, rec.at[:, pl.ds(spots, spots)], sem.at[1]),
+    dests = out_re.shape[0]
+
+    def in_copies(e):
+        return [
+            pltpu.make_async_copy(
+                ref.at[first + e, :, pl.ds(h * LANES, LANES)], obj.at[e, c, h], obj_sem.at[e, c, h]
+            )
+            for c, ref in enumerate((o_re, o_im))
+            for h in range(2)
+        ] + [
+            pltpu.make_async_copy(own_rec.at[first + e], rec.at[e, pl.ds(0, spots)], rec_sem.at[e, 0]),
+            pltpu.make_async_copy(par_rec.at[e], rec.at[e, pl.ds(spots, spots)], rec_sem.at[e, 1]),
+        ]
+
+    def out_copies(e):
+        return [
+            pltpu.make_async_copy(stage.at[e, c], ref.at[:, e], out_sem.at[e, c])
+            for c, ref in enumerate((out_re, out_im))
+        ]
+
+    shared = [
+        pltpu.make_async_copy(src, dst, shared_sem.at[n])
+        for n, (src, dst) in enumerate(
+            (
+                (pr_hbm.at[pl.ds(first, n_e)], pr_ref),
+                (pi_hbm.at[pl.ds(first, n_e)], pi_ref),
+                (tw_hbm, tw_ref),
+                (wf_hbm, wf_ref),
+                (wb_hbm, wb_ref),
+            )
+        )
     ]
-    for c in copies:
+    for c in in_copies(0) + shared:
         c.start()
+    for e in range(1, n_e):
+        for c in in_copies(e):
+            c.start()
     lane = lax.broadcasted_iota(jnp.int32, (SUBS, LANES), 1)
     block = lane // width
-    acc[...] = jnp.zeros_like(acc)
+    for c in shared:
+        c.wait()
 
     def place(e, index):
-        count = own_count[first + e]
-        mine = index < count
-        slot = jnp.where(mine, index, index - count)
-        slot = jnp.clip(slot, 0, spots - 1)
-        at = ((first + e) * spots + slot) * 2
-        row = jnp.where(mine, own_corner[at], par_corner[at])
-        col = jnp.where(mine, own_corner[at + 1], par_corner[at + 1])
-        return jnp.where(mine, slot, slot + spots), row, col
+        packed = table_ref[(first + e) * used + index]
+        rest = packed % (side * side)
+        return packed // (side * side), rest // side, rest % side
 
     def merge(parts):
         out = parts[0]
@@ -111,112 +141,89 @@
             out = jnp.where(block == n, parts[n], out)
         return out
 
-    def extract(n, carry):
-        e, g = n // groups, n % groups
-        for s in range(SUBS):
-            _, row, col = place(e, g * SUBS + s)
+    def row_of(ref, *index):
+        return jnp.broadcast_to(ref[index], (SUBS, LANES))
+
+    def product(x, w_ref):
+        hi, lo = split_bf16(x)
+        dot = functools.partial(jnp.dot, preferred_element_type=jnp.float32)
+        return dot(hi, w_ref[0]) + dot(lo, w_ref[0]) + dot(hi, w_ref[1])
+
+    def energy(e, carry):
+        acc[...] = jnp.zeros_like(acc)
+        for c in in_copies(e):
+            c.wait()
+        for s in range(used):
+            slot, row, col = place(e, s)
             low = lane >= col
-            to = pl.multiple_of((n * SUBS + s) * SUBS, SUBS)
-            for left, right, dst in ((re0, re1, patch_re), (im0, im1, patch_im)):
+            for c in range(2):
                 parts = []
                 for i in range(fold):
                     at = pl.ds(row + i, SUBS, stride=fold)
-                    v = jnp.where(low, left[e, at, :], right[e, at, :])
+                    v = jnp.where(low, obj[e, c, 0, at, :], obj[e, c, 1, at, :])
                     parts.append(pltpu.roll(v, (i * width - col) & (LANES - 1), 1))
-                dst[pl.ds(to, SUBS), :] = merge(parts)
-        return carry
-
-    lax.fori_loop(0, n_e * groups, extract, 0)
-    for c in copies:
-        c.wait()
-
-    def roots(n, carry):
-        e, g = n // groups, n % groups
-        for s in range(SUBS):
-            slot, _, _ = place(e, g * SUBS + s)
-            to = pl.multiple_of((n * SUBS + s) * SUBS, SUBS)
-            v = jnp.concatenate(
+                patch[c, s * SUBS:(s + 1) * SUBS, :] = merge(parts)
+            root[s * SUBS:(s + 1) * SUBS, :] = jnp.concatenate(
                 [rec[e, slot, r * SUBS:(r + 1) * SUBS, :] for r in range(fold)], axis=1
             )
-            root[pl.ds(to, SUBS), :] = jnp.sqrt(v)
-        return carry
-
-    lax.fori_loop(0, n_e * groups, roots, 0)
-
-    def row_of(ref, *index):
-        return jnp.broadcast_to(ref[index], (SUBS, LANES))
-
-    def multiply(w_ref):
-        for q in range(SUBS):
-            hi, lo = split_bf16(work[q])
-            dot = functools.partial(jnp.dot, preferred_element_type=jnp.float32)
-            work[q] = dot(hi, w_ref[0]) + dot(lo, w_ref[0]) + dot(hi, w_ref[1])
-
-    def energy(e, carry):
-        def forward(g, carry):
-            base = (e * groups + g) * SUBS * SUBS
-            o_re, o_im = [], []
-            for t in range(SUBS):
-                at = pl.ds(base + t, SUBS, stride=SUBS)
-                o_re.append(patch_re[at, :])
-                o_im.append(patch_im[at, :])
+
+        for g in range(groups):
+            base = g * SUBS * SUBS
+            ats = [pl.ds(base + t, SUBS, stride=SUBS) for t in range(SUBS)]
+            w_re = [patch[0, at, :] for at in ats]
+            w_im = [patch[1, at, :] for at in ats]
             for m in range(modes):
                 x_re, x_im = [], []
                 for t in range(SUBS):
                     p_re = row_of(pr_ref, e, m, pl.ds(t, 1), slice(None))
                     p_im = row_of(pi_ref, e, m, pl.ds(t, 1), slice(None))
-                    x_re.append(p_re * o_re[t] - p_im * o_im[t])
-                    x_im.append(p_re * o_im[t] + p_im * o_re[t])
+                    x_re.append(p_re * w_re[t] - p_im * w_im[t])
+                    x_im.append(p_re * w_im[t] + p_im * w_re[t])
                 y_re, y_im = fft8(x_re, x_im, -1)
-                to = pl.ds(pl.multiple_of(g * per_group + m * SUBS, SUBS), SUBS)
                 for q in range(SUBS):
                     a, b = y_re[q], y_im[q]
                     if q:
                         c = row_of(tw_ref, pl.ds(q, 1), slice(None))
                         d = row_of(tw_ref, pl.ds(SUBS + q, 1), slice(None))
                         a, b = a * c - b * d, a * d + b * c
-                    work[q, to, 0:LANES] = a
-                    work[q, to, LANES:2 * LANES] = b
-            return carry
-
-        lax.fori_loop(0, groups, forward, 0)
-        multiply(wf_ref)
-
-        def scale(g, carry):
-            base = (e * groups + g) * SUBS * SUBS
-            for q in range(SUBS):
-                tos = [
-                    pl.ds(pl.multiple_of(g * per_group + m * SUBS, SUBS), SUBS)
-                    for m in range(modes)
-                ]
-                f = [(work[q, to, 0:LANES], work[q, to, LANES:2 * LANES]) for to in tos]
-                power = f[0][0] * f[0][0] + f[0][1] * f[0][1]
-                for a, b in f[1:]:
-                    power = power + a * a + b * b
-                sq = root[pl.ds(base + q, SUBS, stride=SUBS), :]
-                factor = 1.0 - sq * lax.rsqrt(jnp.maximum(power, FLOOR_POWER))
-                for to, (a, b) in zip(tos, f):
-                    work[q, to, 0:LANES] = a * factor
-                    work[q, to, LANES:2 * LANES] = b * factor
-            return carry
-
-        lax.fori_loop(0, groups, scale, 0)
-        multiply(wb_ref)
+                    to = q * per_q + g * per_group + m * SUBS
+                    work[to:to + SUBS, 0:LANES] = a
+                    work[to:to + SUBS, LANES:2 * LANES] = b
+
+        for part in range(2):
+            qs = range(part * SUBS // 2, (part + 1) * SUBS // 2)
+            rows = slice(qs[0] * per_q, (qs[-1] + 1) * per_q)
+            z = product(work[rows, :], wf_ref)
+            scaled = []
+            for q in qs:
+                for g in range(groups):
+                    f = []
+                    for m in range(modes):
+                        at = (q - qs[0]) * per_q + g * per_group + m * SUBS
+                        f.append((z[at:at + SUBS, 0:LANES], z[at:at + SUBS, LANES:2 * LANES]))
+                    power = f[0][0] * f[0][0] + f[0][1] * f[0][1]
+                    for a, b in f[1:]:
+                        power = power + a * a + b * b
+                    measured = root[pl.ds(g * SUBS * SUBS + q, SUBS, stride=SUBS), :]
+                    factor = 1.0 - jnp.sqrt(measured) * lax.rsqrt(jnp.maximum(power, FLOOR_POWER))
+                    scaled += [
+                        jnp.concatenate([a * factor, b * factor], axis=1) for a, b in f
+                    ]
+            work[rows, :] = product(jnp.concatenate(scaled, axis=0), wb_ref)
 
         light = jnp.zeros((SUBS, LANES), jnp.float32)
         for m in range(modes):
             a, b = pr_ref[e, m], pi_ref[e, m]
             light = light + a * a + b * b
 
-        def backward(g, carry):
-            base = (e * groups + g) * SUBS * SUBS
+        for g in range(groups):
             t_re = [None] * SUBS
             t_im = [None] * SUBS
             for m in range(modes):
-                frm = pl.ds(pl.multiple_of(g * per_group + m * SUBS, SUBS), SUBS)
                 x_re, x_im = [], []
                 for q in range(SUBS):
-                    a, b = work[q, frm, 0:LANES], work[q, frm, LANES:2 * LANES]
+                    frm = q * per_q + g * per_group + m * SUBS
+                    a, b = work[frm:frm + SUBS, 0:LANES], work[frm:frm + SUBS, LANES:2 * LANES]
                     if q:
                         c = row_of(tw_ref, pl.ds(q, 1), slice(None))
                         d = row_of(tw_ref, pl.ds(SUBS + q, 1), slice(None))
@@ -232,46 +239,55 @@
                     t_re[t] = a if m == 0 else t_re[t] + a
                     t_im[t] = b if m == 0 else t_im[t] + b
             for t in range(SUBS):
-                at = pl.ds(base + t, SUBS, stride=SUBS)
-                patch_re[at, :] = t_re[t]
-                patch_im[at, :] = t_im[t]
-            for s in range(SUBS):
-                _, row, col = place(e, g * SUBS + s)
-                frm = pl.ds(pl.multiple_of(base + s * SUBS, SUBS), SUBS)
-                terms = (patch_re[frm, :], patch_im[frm, :], light)
-                away = [lane + h * LANES - col for h in range(2)]
-                inside = [(a >= 0) & (a < width) for a in away]
+                at = pl.ds(g * SUBS * SUBS + t, SUBS, stride=SUBS)
+                term[0, at, :] = t_re[t]
+                term[1, at, :] = t_im[t]
+
+        for s in range(used):
+            _, row, col = place(e, s)
+            frm = slice(s * SUBS, (s + 1) * SUBS)
+            terms = (term[0, frm, :], term[1, frm, :], light)
+            which = jnp.where(col <= LANES - width, 0, jnp.where(col >= LANES, 1, 2))
+            start = jnp.where(col <= LANES - width, col, jnp.where(col >= LANES, col - LANES, col - LANES // 2))
+            inside = (lane >= start) & (lane < start + width)
+            ats = [pl.ds(row + i, SUBS, stride=fold) for i in range(fold)]
+            sums = []
+            for n, t in enumerate(terms):
                 for i in range(fold):
-                    at = pl.ds(row + i, SUBS, stride=fold)
-                    for n, term in enumerate(terms):
-                        v = pltpu.roll(term, (col - i * width) & (LANES - 1), 1)
-                        for h in range(2):
-                            acc[n, h, e, at, :] = acc[n, h, e, at, :] + jnp.where(inside[h], v, 0.0)
+                    v = pltpu.roll(t, (start - i * width) & (LANES - 1), 1)
+                    sums.append(acc[which, n, ats[i], :] + jnp.where(inside, v, 0.0))
+            for n in range(3):
+                for i in range(fold):
+                    acc[which, n, ats[i], :] = sums[n * fold + i]
+
+        high = lane >= LANES // 2
+
+        def finish(k, carry):
+            for u in range(2):
+                n = k * 2 + u
+                at = pl.ds(pl.multiple_of(n * SUBS, SUBS), SUBS)
+                dest, far = n % dests, n // dests
+                mid = [pltpu.roll(acc[2, c, at, :], LANES // 2, 1) for c in range(3)]
+                for h in range(2):
+                    mine = high if h == 0 else ~high
+                    full = [acc[h, c, at, :] + jnp.where(mine, mid[c], 0.0) for c in range(3)]
+                    share = 1.0 / (full[2] + REGULARIZER)
+                    for c in range(2):
+                        stage[e, c, dest, far, h] = obj[e, c, h, at, :] - full[c] * share
             return carry
 
-        lax.fori_loop(0, groups, backward, 0)
+        lax.fori_loop(0, side // SUBS // 2, finish, 0)
+        for c in out_copies(e):
+            c.start()
         return carry
 
     lax.fori_loop(0, n_e, energy, 0)
-
-    side = re0.shape[1]
-
-    dests = out_re.shape[0]
-
-    def finish(n, carry):
-        at = pl.ds(pl.multiple_of(n * SUBS, SUBS), SUBS)
-        dest, far = n % dests, n // dests
-        for e in range(n_e):
-            for h, (o_re, o_im) in enumerate(((re0, im0), (re1, im1))):
-                share = 1.0 / (acc[2, h, e, at, :] + REGULARIZER)
-                out_re[dest, e, far, h] = o_re[e, at, :] - acc[0, h, e, at, :] * share
-                out_im[dest, e, far, h] = o_im[e, at, :] - acc[1, h, e, at, :] * share
-        return carry
-
-    lax.fori_loop(0, side // SUBS, finish, 0)
-
-
-def gradient_step(objects, beams, own_rec, par_rec, own_corner, par_corner, own_count, first, n_e, used, fars):
+    for e in range(n_e):
+        for c in out_copies(e):
+            c.wait()
+
+
+def gradient_step(objects, beams, own_rec, par_rec, table, first, n_e, used, fars):
     o_re, o_im = objects
     local, side, _ = o_re.shape
     modes, width = beams[0].shape[1], beams[0].shape[-1]
@@ -280,41 +296,51 @@
     assert flat == SUBS and side == 2 * LANES and used % SUBS == 0
     wf, wb, tw = transform_tables(width)
     shaped = [b.reshape(local, modes, flat, LANES) for b in beams]
-    part = lambda i, f, *_: (f[0] // n_e, 0, 0, 0)
-    half = [pl.BlockSpec((n_e, side, LANES), lambda i, f, *_, h=h: (f[0] // n_e, 0, h)) for h in range(2)]
-    beam_spec = pl.BlockSpec((n_e, modes, flat, LANES), part)
-    whole = pl.BlockSpec(memory_space=pltpu.VMEM)
-    rows = used * modes
-    n = n_e * used * SUBS
+    hbm = pl.BlockSpec(memory_space=pl.ANY)
     out_shape = (side // SUBS // fars, n_e, fars, side // LANES, SUBS, LANES)
     return pl.pallas_call(
         functools.partial(step_kernel, n_e, spots, used, modes, width),
         out_shape=[jax.ShapeDtypeStruct(out_shape, jnp.float32)] * 2,
         grid_spec=pltpu.PrefetchScalarGridSpec(
-            num_scalar_prefetch=4,
+            num_scalar_prefetch=2,
             grid=(1,),
-            in_specs=[
-                half[0], half[1], half[0], half[1], beam_spec, beam_spec,
-                pl.BlockSpec(memory_space=pl.ANY), pl.BlockSpec(memory_space=pl.ANY),
-                whole, whole, whole,
-            ],
-            out_specs=[pl.BlockSpec(out_shape, lambda i, *_: (0,) * len(out_shape))] * 2,
+            in_specs=[hbm] * 9,
+            out_specs=[hbm, hbm],
             scratch_shapes=[
+                pltpu.VMEM((n_e, 2, 2, side, LANES), jnp.float32),
                 pltpu.VMEM((n_e, 2 * spots, width, width), jnp.float32),
-                pltpu.VMEM((n, LANES), jnp.float32),
-                pltpu.VMEM((n, LANES), jnp.float32),
-                pltpu.VMEM((n, LANES), jnp.float32),
-                pltpu.VMEM((SUBS, rows, 2 * LANES), jnp.float32),
-                pltpu.VMEM((3, 2, n_e, side, LANES), jnp.float32),
-                pltpu.VMEM((SUBS, LANES), jnp.float32),
-                pltpu.SemaphoreType.DMA((2,)),
+                *[pltpu.VMEM((n_e, modes, flat, LANES), jnp.float32)] * 2,
+                *[pltpu.VMEM(wf.shape, jnp.bfloat16)] * 2,
+                pltpu.VMEM(tw.shape, jnp.float32),
+                pltpu.VMEM((2, used * SUBS, LANES), jnp.float32),
+                pltpu.VMEM((2, used * SUBS, LANES), jnp.float32),
+                pltpu.VMEM((used * SUBS, LANES), jnp.float32),
+                pltpu.VMEM((SUBS * used * modes, 2 * LANES), jnp.float32),
+                pltpu.VMEM((3, 3, side, LANES), jnp.float32),
+                pltpu.VMEM((n_e, 2, *(out_shape[:1] + out_shape[2:])), jnp.float32),
+                pltpu.SemaphoreType.DMA((n_e, 2, 2)),
+                pltpu.SemaphoreType.DMA((n_e, 2)),
+                pltpu.SemaphoreType.DMA((5,)),
+                pltpu.SemaphoreType.DMA((n_e, 2)),
             ],
         ),
+        compiler_params=pltpu.CompilerParams(vmem_limit_bytes=LARGE),
         name="gradient_step",
     )(
-        first, own_corner, par_corner, own_count,
-        o_re, o_re, o_im, o_im, *shaped, own_rec, par_rec, jnp.asarray(wf), jnp.asarray(wb), jnp.asarray(tw),
+        first, table, o_re, o_im, *shaped, own_rec, par_rec,
+        jnp.asarray(wf), jnp.asarray(wb), jnp.asarray(tw),
     )
+
+
+def slot_table(corners, counts, side, used, swap):
+    local, spots, _ = corners.shape
+    packed = corners[..., 0] * side + corners[..., 1]
+    both = jnp.concatenate([packed, lax.ppermute(packed, "ta", swap)], axis=1)
+    both = both + jnp.arange(2 * spots, dtype=jnp.int32) * (side * side)
+    index = jnp.arange(used, dtype=jnp.int32)[None]
+    index = index + jnp.where(index < counts, 0, spots - counts)
+    chosen = index[:, :, None] == jnp.arange(2 * spots, dtype=jnp.int32)
+    return jnp.sum(jnp.where(chosen, both[:, None, :], 0), axis=2).reshape(-1)
 
 
 def dot3(a, b):
@@ -447,16 +473,13 @@
     first = tile * n_e if divided else jnp.zeros((), jnp.int32)
     give = lax.dynamic_slice_in_dim(own_rec, (1 - tile) * n_e, n_e, 0) if divided else own_rec
     par_rec = lax.ppermute(give, "ta", swap)
-    own_corner = window_corners.reshape(-1)
-    par_corner = lax.ppermute(own_corner, "ta", swap)
+    table = slot_table(window_corners[:, 0], filled_tallies, side, used, swap)
     stepped = gradient_step(
         (sample_inphase, sample_quadrature),
         (beam_inphase, beam_quadrature),
         own_rec,
         par_rec,
-        own_corner,
-        par_corner,
-        filled_tallies.reshape(-1),
+        table,
         first.astype(jnp.int32)[None],
         n_e,
         used,

time: 118 us -> 116 us (0.983)
  Pallas kernels: 26.5 us -> 23.8 us
    pallas_call x1, Pallas kernels: 19.5 us -> 16.8 us  [gradient_step(): pl.pallas_call(functools.partial(step_kernel, n_e, spots, used, modes, wi...]
  transfers between devices with their start and end apart: 8 -> 8, of which waited for: 7 -> 6; matrix products, arithmetic and copies ran while one was open for 6% -> 8% of each run, Pallas kernels for 5% -> 5%
where the time goes in v4:
time: 116 us
  waiting for transfers between devices  56.7 us (49%)
  Pallas kernels  23.8 us (21%)
  starting transfers between devices  23.1 us (20%)
  local copies, waits for them, and re-layouts  5.61 us (5%)
  other arithmetic  5.19 us (4%)
    ppermute x2, waiting for transfers between devices, local(): theirs = lax.ppermute(mine, 'far', swap)  30.5 us
    pallas_call x1, Pallas kernels, gradient_step(): pl.pallas_call(functools.partial(step_kernel, n_e, spots, used, modes, wi...  16.8 us
    all_to_all x2, waiting for transfers between devices, local(): lax.all_to_all(x, ('cube', 'ta'), 0, 0, tiled=True)  13.5 us
    all_to_all x2, waiting for transfers between devices, local(): lax.all_to_all(fit.reshape(cube, local_energies, fars, pix // LANES, LANE...  12.8 us
    all_to_all x2, starting transfers between devices, local(): lax.all_to_all(fit.reshape(cube, local_energies, fars, pix // LANES, LANE...  9.97 us
    all_to_all x2, starting transfers between devices, local(): lax.all_to_all(x, ('cube', 'ta'), 0, 0, tiled=True)  9.97 us
    pallas_call x2, Pallas kernels, fitted_values(): pl.pallas_call(fit_kernel, out_shape=[jax.ShapeDtypeStruct((edges, own),...  3.58 us
    ppermute x2, starting transfers between devices, local(): theirs = lax.ppermute(mine, 'far', swap)  2.6 us
  transfers between devices with their start and end apart: 8, of which 6 were waited for; matrix products, arithmetic and copies ran while one was open for 8% of the time, Pallas kernels for 5%

profile of v4, /device:TPU:0, one launch (start us, length us, event | category | flops | bytes accessed | tf_op | source)
XLA Modules:
  0.0 115.7 jit_solution(556912286156141637)
XLA Ops:
  0.7 0.8 copy.24
  1.5 0.5 collective-permute-start
  1.9 1.3 %dynamic-slice_bitcast_fusion = f32[4,16,32,32]{3,2,1,0:T(8,128)S(1)} fusion(f32[8,1,16,32,32]{4,3,2,1,0:T(8,128)} %param.15, s32[]{:T(128)S(6)} %select_n.25), kind=kLoop, calls=%fused_computation | loop fusion | bytes 524292 | tf_op jit(solution)/shard_map/dynamic_slice | solution.py:474
  3.4 0.8 reshape.123.pr_hbm
  4.2 0.8 reshape.124.pi_hbm
  5.1 0.3 select_reduce_fusion
  5.4 0.7 reshape.122.table_ref
  6.0 1.0 copy-done.1
  7.0 16.8 %gradient_step.1 = (f32[16,4,2,2,8,128]{5,4,3,2,1,0:T(8,128)}, f32[16,4,2,2,8,128]{5,4,3,2,1,0:T(8,128)}) custom-call(s32[1]{0:T(128)} %bitcast.1.first_ref, s32[192]{0:T(256)} %reshape.122.table_ref, f32[8,256,256]{2,1,0:T(8,128)} %o_re.1, f32[8,256,256]{2,1,0:T(8,128)} %o_im.1, f32[8,3,8,128]{3,2,1,0:T(8,128)} %reshape.123.pr_hbm, ...), custom_call_target="tpu_custom_call" | custom-call | tf_op jit(solution)/shard_map/gradient_step/pallas_call | solution.py:301
  23.8 6.3 %all-to-all-start.2 = ((f32[16,4,2,2,8,128]{5,4,3,2,1,0:T(8,128)}), f32[16,4,2,2,8,128]{5,4,3,2,1,0:T(8,128)S(1)}, u32[]{:S(2)}, u32[]{:S(2)}) async-start(f32[16,4,2,2,8,128]{5,4,3,2,1,0:T(8,128)} %get-tuple-element.16), calls=%async_computation.2 | async-start | bytes 2097152 | tf_op jit(solution)/shard_map/all_to_all | solution.py:504
  30.4 1.5 %cholesky.16 = f32[16,16]{1,0:T(8,128)S(1)} custom-call(f32[16,16]{1,0:T(8,128)S(1)} %fusion.5), custom_call_target="Cholesky" | custom-call | tf_op jit(solution)/shard_map/jit(cholesky)/cholesky | solution.py:489
  31.9 0.6 compare_reduce_fusion
  32.5 0.6 fusion
  33.2 1.2 %custom-call.10 = f32[1,16,16]{1,2,0:T(8,128)S(1)} custom-call(f32[1,16,16]{2,1,0:T(8,128)S(1)} %fusion), custom_call_target="InvertDiagBlocksLowerTriangular" | custom-call | tf_op jit(solution)/shard_map/jit(_cho_solve)/triangular_solve | solution.py:490
  34.6 0.2 fusion.3
  35.0 11.3 %all-to-all-done.2 = f32[16,4,2,2,8,128]{5,4,3,2,1,0:T(8,128)S(1)} async-done(((f32[16,4,2,2,8,128]{5,4,3,2,1,0:T(8,128)}), f32[16,4,2,2,8,128]{5,4,3,2,1,0:T(8,128)S(1)}, u32[]{:S(2)}, u32[]{:S(2)}) %all-to-all-start.2) | async-done | bytes 1048608 | tf_op jit(solution)/shard_map/all_to_all | solution.py:504
  46.3 3.7 %all-to-all-start = ((f32[16,4,2,2,8,128]{5,4,3,2,1,0:T(8,128)}), f32[16,4,2,2,8,128]{5,4,3,2,1,0:T(8,128)S(1)}, u32[]{:S(2)}, u32[]{:S(2)}) async-start(f32[16,4,2,2,8,128]{5,4,3,2,1,0:T(8,128)} %get-tuple-element.13), calls=%async_computation | async-start | bytes 2097152 | tf_op jit(solution)/shard_map/all_to_all | solution.py:504
  50.0 0.7 partial_coefs.3.mine_ref
  50.6 2.6 %collective-permute-start.3 = (f32[16,4096]{1,0:T(8,128)S(1)}, f32[16,4096]{1,0:T(8,128)S(1)}, u32[]{:S(2)}, u32[]{:S(2)}) collective-permute-start(f32[16,4096]{1,0:T(8,128)S(1)} %partial_coefs.3.mine_ref), channel_id=1, source_target_pairs={{0,16},{16,0},{1,17},{17,1},{2,18},{18,2},{3,19},{19,3},{4,20},{20... | collective-permute-start | bytes 786440 | tf_op jit(solution)/shard_map/ppermute | solution.py:507
  53.2 14.5 %collective-permute-done.3.theirs_ref = f32[16,4096]{1,0:T(8,128)S(1)} collective-permute-done((f32[16,4096]{1,0:T(8,128)S(1)}, f32[16,4096]{1,0:T(8,128)S(1)}, u32[]{:S(2)}, u32[]{:S(2)}) %collective-permute-start.3) | collective-permute-done | bytes 262176 | tf_op jit(solution)/shard_map/ppermute | solution.py:507
  67.7 1.8 %fitted_values.3 = (f32[16,2048]{1,0:T(8,128)S(1)}, f32[2048,128]{1,0:T(8,128)}) custom-call(s32[1]{0:T(128)} %bitcast.far_ref, f32[16,4096]{1,0:T(8,128)S(1)} %partial_coefs.3.mine_ref, f32[16,4096]{1,0:T(8,128)S(1)} %collective-permute-done.3.theirs_ref, f32[64,16]{1,0:T(8,128)S(1)} %bitcast.42), custom_call_target="tpu_custom_call" | custom-call | flops 25165824 | bytes 1048576 | tf_op jit(solution)/shard_map/fitted_values/pallas_call | solution.py:403
  69.5 2.2 %all-to-all-done = f32[16,4,2,2,8,128]{5,4,3,2,1,0:T(8,128)S(1)} async-done(((f32[16,4,2,2,8,128]{5,4,3,2,1,0:T(8,128)}), f32[16,4,2,2,8,128]{5,4,3,2,1,0:T(8,128)S(1)}, u32[]{:S(2)}, u32[]{:S(2)}) %all-to-all-start) | async-done | bytes 1048608 | tf_op jit(solution)/shard_map/all_to_all | solution.py:504
  71.7 5.7 %all-to-all-start.3 = ((f32[8,8,2,16,128]{4,3,2,1,0:T(8,128)}), f32[8,8,2,16,128]{4,3,2,1,0:T(8,128)S(1)}, u32[]{:S(2)}, u32[]{:S(2)}) async-start(f32[8,8,2,16,128]{4,3,2,1,0:T(8,128)} %bitcast.15), calls=%async_computation.3 | async-start | bytes 2097152 | tf_op jit(solution)/shard_map/all_to_all | solution.py:510
  77.3 0.7 partial_coefs.2.mine_ref
  78.0 16.0 %collective-permute-done.2.theirs_ref = f32[16,4096]{1,0:T(8,128)S(1)} collective-permute-done((f32[16,4096]{1,0:T(8,128)S(1)}, f32[16,4096]{1,0:T(8,128)S(1)}, u32[]{:S(2)}, u32[]{:S(2)}) %collective-permute-start.2) | collective-permute-done | bytes 262176 | tf_op jit(solution)/shard_map/ppermute | solution.py:507
  94.1 1.8 %fitted_values.2 = (f32[16,2048]{1,0:T(8,128)S(1)}, f32[2048,128]{1,0:T(8,128)}) custom-call(s32[1]{0:T(128)} %bitcast.far_ref, f32[16,4096]{1,0:T(8,128)S(1)} %partial_coefs.2.mine_ref, f32[16,4096]{1,0:T(8,128)S(1)} %collective-permute-done.2.theirs_ref, f32[64,16]{1,0:T(8,128)S(1)} %bitcast.43), custom_call_target="tpu_custom_call" | custom-call | flops 25165824 | bytes 1048576 | tf_op jit(solution)/shard_map/fitted_values/pallas_call | solution.py:403
  95.9 0.8 all-to-all-done.3.in_ref
  96.7 4.3 %all-to-all-start.1 = ((f32[8,8,2,16,128]{4,3,2,1,0:T(8,128)}), f32[8,8,2,16,128]{4,3,2,1,0:T(8,128)S(1)}, u32[]{:S(2)}, u32[]{:S(2)}) async-start(f32[8,8,2,16,128]{4,3,2,1,0:T(8,128)} %bitcast.13), calls=%async_computation.1 | async-start | bytes 2097152 | tf_op jit(solution)/shard_map/all_to_all | solution.py:510
  101.0 0.7 pad_maximum_fusion
  101.7 1.0 gather_part.2.refs_0_
  102.8 11.9 %all-to-all-done.1.in_ref = f32[8,8,2,16,128]{4,3,2,1,0:T(8,128)S(1)} async-done(((f32[8,8,2,16,128]{4,3,2,1,0:T(8,128)}), f32[8,8,2,16,128]{4,3,2,1,0:T(8,128)S(1)}, u32[]{:S(2)}, u32[]{:S(2)}) %all-to-all-start.1) | async-done | bytes 1048608 | tf_op jit(solution)/shard_map/all_to_all | solution.py:510
  114.7 1.0 gather_part.3
  (26 shorter events, 0.9 us)
Async XLA Ops:
  0.6 29.5 %copy-start = (f32[16,128]{1,0:T(8,128)S(1)}, f32[16,128]{1,0:T(8,128)}, u32[]{:S(2)}) copy-start(f32[16,128]{1,0:T(8,128)} %param.18) | copy-start | bytes 24580
  0.6 2.7 %copy-start.4 = (s32[8,1]{0,1:T(1,128)S(1)}, s32[8,1]{0,1:T(1,128)}, u32[]{:S(2)}) copy-start(s32[8,1]{0,1:T(1,128)} %param.17) | copy-start | bytes 100
  0.7 2.8 %copy-start.2 = (f32[8,3,32,32]{3,2,1,0:T(8,128)S(1)}, f32[8,3,32,32]{3,2,1,0:T(8,128)}, u32[]{:S(2)}) copy-start(f32[8,3,32,32]{3,2,1,0:T(8,128)} %param.13) | copy-start | bytes 294916
  0.7 3.5 %copy-start.3 = (f32[8,3,32,32]{3,2,1,0:T(8,128)S(1)}, f32[8,3,32,32]{3,2,1,0:T(8,128)}, u32[]{:S(2)}) copy-start(f32[8,3,32,32]{3,2,1,0:T(8,128)} %param.14) | copy-start | bytes 294916
  1.5 3.5 %collective-permute-start = (s32[8,16]{1,0:T(8,128)S(1)}, s32[8,16]{1,0:T(8,128)S(1)}, u32[]{:S(2)}, u32[]{:S(2)}) collective-permute-start(s32[8,16]{1,0:T(8,128)S(1)} %fusion.6), channel_id=1, source_target_pairs={{0,1},{1,0},{2,3},{3,2},{4,5},{5,4},{6,7},{7,6},{8,9},{9,8},{10,11... | collective-permute-start | bytes 1544 | tf_op jit(solution)/shard_map/ppermute | solution.py:338
  3.2 2.8 %collective-permute-start.1 = (f32[4,16,32,32]{3,2,1,0:T(8,128)S(1)}, f32[4,16,32,32]{3,2,1,0:T(8,128)S(1)}, u32[]{:S(2)}, u32[]{:S(2)}) collective-permute-start(f32[4,16,32,32]{3,2,1,0:T(8,128)S(1)} %dynamic-slice_bitcast_fusion), channel_id=1, source_target_pairs={{0,1},{1,0},{2,3},{3,2},{4,5},{5,4},{6,7},{7,6},{8,9},{9,8},{10,11... | collective-permute-start | bytes 786440 | tf_op jit(solution)/shard_map/ppermute | solution.py:475
  6.0 1.0 copy-start.1
  23.8 22.5 %all-to-all-start.2 = ((f32[16,4,2,2,8,128]{5,4,3,2,1,0:T(8,128)}), f32[16,4,2,2,8,128]{5,4,3,2,1,0:T(8,128)S(1)}, u32[]{:S(2)}, u32[]{:S(2)}) async-start(f32[16,4,2,2,8,128]{5,4,3,2,1,0:T(8,128)} %get-tuple-element.16), calls=%async_computation.2 | async-start | bytes 2097152 | tf_op jit(solution)/shard_map/all_to_all | solution.py:504
  46.3 25.4 %all-to-all-start = ((f32[16,4,2,2,8,128]{5,4,3,2,1,0:T(8,128)}), f32[16,4,2,2,8,128]{5,4,3,2,1,0:T(8,128)S(1)}, u32[]{:S(2)}, u32[]{:S(2)}) async-start(f32[16,4,2,2,8,128]{5,4,3,2,1,0:T(8,128)} %get-tuple-element.13), calls=%async_computation | async-start | bytes 2097152 | tf_op jit(solution)/shard_map/all_to_all | solution.py:504
  50.6 17.1 %collective-permute-start.3 = (f32[16,4096]{1,0:T(8,128)S(1)}, f32[16,4096]{1,0:T(8,128)S(1)}, u32[]{:S(2)}, u32[]{:S(2)}) collective-permute-start(f32[16,4096]{1,0:T(8,128)S(1)} %partial_coefs.3.mine_ref), channel_id=1, source_target_pairs={{0,16},{16,0},{1,17},{17,1},{2,18},{18,2},{3,19},{19,3},{4,20},{20... | collective-permute-start | bytes 786440 | tf_op jit(solution)/shard_map/ppermute | solution.py:507
  71.7 25.0 %all-to-all-start.3 = ((f32[8,8,2,16,128]{4,3,2,1,0:T(8,128)}), f32[8,8,2,16,128]{4,3,2,1,0:T(8,128)S(1)}, u32[]{:S(2)}, u32[]{:S(2)}) async-start(f32[8,8,2,16,128]{4,3,2,1,0:T(8,128)} %bitcast.15), calls=%async_computation.3 | async-start | bytes 2097152 | tf_op jit(solution)/shard_map/all_to_all | solution.py:510
  78.0 16.0 %collective-permute-start.2 = (f32[16,4096]{1,0:T(8,128)S(1)}, f32[16,4096]{1,0:T(8,128)S(1)}, u32[]{:S(2)}, u32[]{:S(2)}) collective-permute-start(f32[16,4096]{1,0:T(8,128)S(1)} %partial_coefs.2.mine_ref), channel_id=1, source_target_pairs={{0,16},{16,0},{1,17},{17,1},{2,18},{18,2},{3,19},{19,3},{4,20},{20... | collective-permute-start | bytes 786440 | tf_op jit(solution)/shard_map/ppermute | solution.py:507
  96.7 18.0 %all-to-all-start.1 = ((f32[8,8,2,16,128]{4,3,2,1,0:T(8,128)}), f32[8,8,2,16,128]{4,3,2,1,0:T(8,128)S(1)}, u32[]{:S(2)}, u32[]{:S(2)}) async-start(f32[8,8,2,16,128]{4,3,2,1,0:T(8,128)} %bitcast.13), calls=%async_computation.1 | async-start | bytes 2097152 | tf_op jit(solution)/shard_map/all_to_all | solution.py:510

commit v5 on v4

--- a/solution.py
+++ b/solution.py
@@ -38,7 +38,7 @@
     def halves(a):
         hi = a.astype(jnp.bfloat16)
         lo = (a - hi.astype(np.float64)).astype(jnp.bfloat16)
-        return np.stack([hi, lo])
+        return np.concatenate([hi, hi, lo])
 
     return halves(real), halves(real.T.copy()), tw
 
@@ -79,7 +79,7 @@
     first_ref, table_ref,
     o_re, o_im, pr_hbm, pi_hbm, own_rec, par_rec, wf_hbm, wb_hbm, tw_hbm,
     out_re, out_im,
-    obj, rec, pr_ref, pi_ref, wf_ref, wb_ref, tw_ref, patch, term, root, work, acc, stage,
+    obj, rec, pr_ref, pi_ref, wf_ref, wb_ref, tw_ref, patch, term, root, work, sum_re, sum_im, sum_light, stage,
     obj_sem, rec_sem, shared_sem, out_sem,
 ):
     fold = LANES // width
@@ -89,6 +89,7 @@
     side = obj.shape[3]
     first = first_ref[0]
     dests = out_re.shape[0]
+    sums = (sum_re, sum_im, sum_light)
 
     def in_copies(e):
         return [
@@ -132,8 +133,8 @@
 
     def place(e, index):
         packed = table_ref[(first + e) * used + index]
-        rest = packed % (side * side)
-        return packed // (side * side), rest // side, rest % side
+        shift = side.bit_length() - 1
+        return packed >> (2 * shift), (packed >> shift) & (side - 1), packed & (side - 1)
 
     def merge(parts):
         out = parts[0]
@@ -146,11 +147,12 @@
 
     def product(x, w_ref):
         hi, lo = split_bf16(x)
-        dot = functools.partial(jnp.dot, preferred_element_type=jnp.float32)
-        return dot(hi, w_ref[0]) + dot(lo, w_ref[0]) + dot(hi, w_ref[1])
+        wide = jnp.concatenate([hi, lo, hi], axis=1)
+        return jnp.dot(wide, w_ref[...], preferred_element_type=jnp.float32)
 
     def energy(e, carry):
-        acc[...] = jnp.zeros_like(acc)
+        for acc in sums:
+            acc[...] = jnp.zeros_like(acc)
         for c in in_copies(e):
             c.wait()
         for s in range(used):
@@ -251,32 +253,31 @@
             start = jnp.where(col <= LANES - width, col, jnp.where(col >= LANES, col - LANES, col - LANES // 2))
             inside = (lane >= start) & (lane < start + width)
             ats = [pl.ds(row + i, SUBS, stride=fold) for i in range(fold)]
-            sums = []
-            for n, t in enumerate(terms):
+            for acc, t in zip(sums, terms):
+                new = []
                 for i in range(fold):
                     v = pltpu.roll(t, (start - i * width) & (LANES - 1), 1)
-                    sums.append(acc[which, n, ats[i], :] + jnp.where(inside, v, 0.0))
-            for n in range(3):
+                    new.append(acc[which, ats[i], :] + jnp.where(inside, v, 0.0))
                 for i in range(fold):
-                    acc[which, n, ats[i], :] = sums[n * fold + i]
+                    acc[which, ats[i], :] = new[i]
 
         high = lane >= LANES // 2
 
         def finish(k, carry):
-            for u in range(2):
-                n = k * 2 + u
+            for u in range(SUBS):
+                n = k * SUBS + u
                 at = pl.ds(pl.multiple_of(n * SUBS, SUBS), SUBS)
                 dest, far = n % dests, n // dests
-                mid = [pltpu.roll(acc[2, c, at, :], LANES // 2, 1) for c in range(3)]
+                mid = [pltpu.roll(acc[2, at, :], LANES // 2, 1) for acc in sums]
                 for h in range(2):
                     mine = high if h == 0 else ~high
-                    full = [acc[h, c, at, :] + jnp.where(mine, mid[c], 0.0) for c in range(3)]
+                    full = [acc[h, at, :] + jnp.where(mine, m, 0.0) for acc, m in zip(sums, mid)]
                     share = 1.0 / (full[2] + REGULARIZER)
                     for c in range(2):
                         stage[e, c, dest, far, h] = obj[e, c, h, at, :] - full[c] * share
             return carry
 
-        lax.fori_loop(0, side // SUBS // 2, finish, 0)
+        lax.fori_loop(0, side // SUBS // SUBS, finish, 0)
         for c in out_copies(e):
             c.start()
         return carry
@@ -316,7 +317,7 @@
                 pltpu.VMEM((2, used * SUBS, LANES), jnp.float32),
                 pltpu.VMEM((used * SUBS, LANES), jnp.float32),
                 pltpu.VMEM((SUBS * used * modes, 2 * LANES), jnp.float32),
-                pltpu.VMEM((3, 3, side, LANES), jnp.float32),
+                *[pltpu.VMEM((3, side, LANES), jnp.float32)] * 3,
                 pltpu.VMEM((n_e, 2, *(out_shape[:1] + out_shape[2:])), jnp.float32),
                 pltpu.SemaphoreType.DMA((n_e, 2, 2)),
                 pltpu.SemaphoreType.DMA((n_e, 2)),

time: 116 us -> 112 us (0.966)
  Pallas kernels: 23.8 us -> 19.6 us
    pallas_call x1, Pallas kernels: 16.8 us -> 12.6 us  [gradient_step(): pl.pallas_call(functools.partial(step_kernel, n_e, spots, used, modes, wi...]
  transfers between devices with their start and end apart: 8 -> 8, of which waited for: 6 -> 6; matrix products, arithmetic and copies ran while one was open for 8% -> 9% of each run, Pallas kernels for 5% -> 5%
where the time goes in v5:
time: 112 us
  waiting for transfers between devices  56.7 us (51%)
  starting transfers between devices  23.2 us (21%)
  Pallas kernels  19.6 us (18%)
  local copies, waits for them, and re-layouts  5.61 us (5%)
  other arithmetic  5.19 us (5%)
    ppermute x2, waiting for transfers between devices, local(): theirs = lax.ppermute(mine, 'far', swap)  30.4 us
    all_to_all x2, waiting for transfers between devices, local(): lax.all_to_all(x, ('cube', 'ta'), 0, 0, tiled=True)  13.5 us
    all_to_all x2, waiting for transfers between devices, local(): lax.all_to_all(fit.reshape(cube, local_energies, fars, pix // LANES, LANE...  12.8 us
    pallas_call x1, Pallas kernels, gradient_step(): pl.pallas_call(functools.partial(step_kernel, n_e, spots, used, modes, wi...  12.6 us
    all_to_all x2, starting transfers between devices, local(): lax.all_to_all(fit.reshape(cube, local_energies, fars, pix // LANES, LANE...  10 us
    all_to_all x2, starting transfers between devices, local(): lax.all_to_all(x, ('cube', 'ta'), 0, 0, tiled=True)  9.97 us
    pallas_call x2, Pallas kernels, fitted_values(): pl.pallas_call(fit_kernel, out_shape=[jax.ShapeDtypeStruct((edges, own),...  3.58 us
    ppermute x2, starting transfers between devices, local(): theirs = lax.ppermute(mine, 'far', swap)  2.62 us
  transfers between devices with their start and end apart: 8, of which 6 were waited for; matrix products, arithmetic and copies ran while one was open for 9% of the time, Pallas kernels for 5%

profile of v5, /device:TPU:0, one launch (start us, length us, event | category | flops | bytes accessed | tf_op | source)
XLA Modules:
  0.0 111.5 jit_solution(13288640883917225122)
XLA Ops:
  0.7 0.8 copy.24
  1.5 0.5 collective-permute-start
  1.9 1.3 %dynamic-slice_bitcast_fusion = f32[4,16,32,32]{3,2,1,0:T(8,128)S(1)} fusion(f32[8,1,16,32,32]{4,3,2,1,0:T(8,128)} %param.15, s32[]{:T(128)S(6)} %select_n.25), kind=kLoop, calls=%fused_computation | loop fusion | bytes 524292 | tf_op jit(solution)/shard_map/dynamic_slice | solution.py:475
  3.4 0.8 reshape.123.pr_hbm
  4.2 0.8 reshape.124.pi_hbm
  5.1 0.3 select_reduce_fusion
  5.4 0.7 reshape.122.table_ref
  6.0 1.0 copy-done.1
  7.0 12.6 %gradient_step.1 = (f32[16,4,2,2,8,128]{5,4,3,2,1,0:T(8,128)}, f32[16,4,2,2,8,128]{5,4,3,2,1,0:T(8,128)}) custom-call(s32[1]{0:T(128)} %bitcast.1.first_ref, s32[192]{0:T(256)} %reshape.122.table_ref, f32[8,256,256]{2,1,0:T(8,128)} %o_re.1, f32[8,256,256]{2,1,0:T(8,128)} %o_im.1, f32[8,3,8,128]{3,2,1,0:T(8,128)} %reshape.123.pr_hbm, ...), custom_call_target="tpu_custom_call" | custom-call | tf_op jit(solution)/shard_map/gradient_step/pallas_call | solution.py:302
  19.7 6.3 %all-to-all-start.2 = ((f32[16,4,2,2,8,128]{5,4,3,2,1,0:T(8,128)}), f32[16,4,2,2,8,128]{5,4,3,2,1,0:T(8,128)S(1)}, u32[]{:S(2)}, u32[]{:S(2)}) async-start(f32[16,4,2,2,8,128]{5,4,3,2,1,0:T(8,128)} %get-tuple-element.16), calls=%async_computation.2 | async-start | bytes 2097152 | tf_op jit(solution)/shard_map/all_to_all | solution.py:505
  26.2 1.5 %cholesky.16 = f32[16,16]{1,0:T(8,128)S(1)} custom-call(f32[16,16]{1,0:T(8,128)S(1)} %fusion.5), custom_call_target="Cholesky" | custom-call | tf_op jit(solution)/shard_map/jit(cholesky)/cholesky | solution.py:490
  27.7 0.6 compare_reduce_fusion
  28.3 0.6 fusion
  29.0 1.2 %custom-call.10 = f32[1,16,16]{1,2,0:T(8,128)S(1)} custom-call(f32[1,16,16]{2,1,0:T(8,128)S(1)} %fusion), custom_call_target="InvertDiagBlocksLowerTriangular" | custom-call | tf_op jit(solution)/shard_map/jit(_cho_solve)/triangular_solve | solution.py:491
  30.4 0.2 fusion.3
  30.8 11.3 %all-to-all-done.2 = f32[16,4,2,2,8,128]{5,4,3,2,1,0:T(8,128)S(1)} async-done(((f32[16,4,2,2,8,128]{5,4,3,2,1,0:T(8,128)}), f32[16,4,2,2,8,128]{5,4,3,2,1,0:T(8,128)S(1)}, u32[]{:S(2)}, u32[]{:S(2)}) %all-to-all-start.2) | async-done | bytes 1048608 | tf_op jit(solution)/shard_map/all_to_all | solution.py:505
  42.1 3.7 %all-to-all-start = ((f32[16,4,2,2,8,128]{5,4,3,2,1,0:T(8,128)}), f32[16,4,2,2,8,128]{5,4,3,2,1,0:T(8,128)S(1)}, u32[]{:S(2)}, u32[]{:S(2)}) async-start(f32[16,4,2,2,8,128]{5,4,3,2,1,0:T(8,128)} %get-tuple-element.13), calls=%async_computation | async-start | bytes 2097152 | tf_op jit(solution)/shard_map/all_to_all | solution.py:505
  45.8 0.7 partial_coefs.3.mine_ref
  46.5 2.6 %collective-permute-start.3 = (f32[16,4096]{1,0:T(8,128)S(1)}, f32[16,4096]{1,0:T(8,128)S(1)}, u32[]{:S(2)}, u32[]{:S(2)}) collective-permute-start(f32[16,4096]{1,0:T(8,128)S(1)} %partial_coefs.3.mine_ref), channel_id=1, source_target_pairs={{0,16},{16,0},{1,17},{17,1},{2,18},{18,2},{3,19},{19,3},{4,20},{20... | collective-permute-start | bytes 786440 | tf_op jit(solution)/shard_map/ppermute | solution.py:508
  49.1 14.4 %collective-permute-done.3.theirs_ref = f32[16,4096]{1,0:T(8,128)S(1)} collective-permute-done((f32[16,4096]{1,0:T(8,128)S(1)}, f32[16,4096]{1,0:T(8,128)S(1)}, u32[]{:S(2)}, u32[]{:S(2)}) %collective-permute-start.3) | collective-permute-done | bytes 262176 | tf_op jit(solution)/shard_map/ppermute | solution.py:508
  63.5 1.8 %fitted_values.3 = (f32[16,2048]{1,0:T(8,128)S(1)}, f32[2048,128]{1,0:T(8,128)}) custom-call(s32[1]{0:T(128)} %bitcast.far_ref, f32[16,4096]{1,0:T(8,128)S(1)} %partial_coefs.3.mine_ref, f32[16,4096]{1,0:T(8,128)S(1)} %collective-permute-done.3.theirs_ref, f32[64,16]{1,0:T(8,128)S(1)} %bitcast.42), custom_call_target="tpu_custom_call" | custom-call | flops 25165824 | bytes 1048576 | tf_op jit(solution)/shard_map/fitted_values/pallas_call | solution.py:404
  65.3 2.2 %all-to-all-done = f32[16,4,2,2,8,128]{5,4,3,2,1,0:T(8,128)S(1)} async-done(((f32[16,4,2,2,8,128]{5,4,3,2,1,0:T(8,128)}), f32[16,4,2,2,8,128]{5,4,3,2,1,0:T(8,128)S(1)}, u32[]{:S(2)}, u32[]{:S(2)}) %all-to-all-start) | async-done | bytes 1048608 | tf_op jit(solution)/shard_map/all_to_all | solution.py:505
  67.5 5.7 %all-to-all-start.3 = ((f32[8,8,2,16,128]{4,3,2,1,0:T(8,128)}), f32[8,8,2,16,128]{4,3,2,1,0:T(8,128)S(1)}, u32[]{:S(2)}, u32[]{:S(2)}) async-start(f32[8,8,2,16,128]{4,3,2,1,0:T(8,128)} %bitcast.15), calls=%async_computation.3 | async-start | bytes 2097152 | tf_op jit(solution)/shard_map/all_to_all | solution.py:511
  73.2 0.7 partial_coefs.2.mine_ref
  73.9 16.0 %collective-permute-done.2.theirs_ref = f32[16,4096]{1,0:T(8,128)S(1)} collective-permute-done((f32[16,4096]{1,0:T(8,128)S(1)}, f32[16,4096]{1,0:T(8,128)S(1)}, u32[]{:S(2)}, u32[]{:S(2)}) %collective-permute-start.2) | collective-permute-done | bytes 262176 | tf_op jit(solution)/shard_map/ppermute | solution.py:508
  89.9 1.8 %fitted_values.2 = (f32[16,2048]{1,0:T(8,128)S(1)}, f32[2048,128]{1,0:T(8,128)}) custom-call(s32[1]{0:T(128)} %bitcast.far_ref, f32[16,4096]{1,0:T(8,128)S(1)} %partial_coefs.2.mine_ref, f32[16,4096]{1,0:T(8,128)S(1)} %collective-permute-done.2.theirs_ref, f32[64,16]{1,0:T(8,128)S(1)} %bitcast.43), custom_call_target="tpu_custom_call" | custom-call | flops 25165824 | bytes 1048576 | tf_op jit(solution)/shard_map/fitted_values/pallas_call | solution.py:404
  91.7 0.8 all-to-all-done.3.in_ref
  92.5 4.3 %all-to-all-start.1 = ((f32[8,8,2,16,128]{4,3,2,1,0:T(8,128)}), f32[8,8,2,16,128]{4,3,2,1,0:T(8,128)S(1)}, u32[]{:S(2)}, u32[]{:S(2)}) async-start(f32[8,8,2,16,128]{4,3,2,1,0:T(8,128)} %bitcast.13), calls=%async_computation.1 | async-start | bytes 2097152 | tf_op jit(solution)/shard_map/all_to_all | solution.py:511
  96.8 0.7 pad_maximum_fusion
  97.6 1.0 gather_part.2.refs_0_
  98.6 11.9 %all-to-all-done.1.in_ref = f32[8,8,2,16,128]{4,3,2,1,0:T(8,128)S(1)} async-done(((f32[8,8,2,16,128]{4,3,2,1,0:T(8,128)}), f32[8,8,2,16,128]{4,3,2,1,0:T(8,128)S(1)}, u32[]{:S(2)}, u32[]{:S(2)}) %all-to-all-start.1) | async-done | bytes 1048608 | tf_op jit(solution)/shard_map/all_to_all | solution.py:511
  110.5 1.0 gather_part.3
  (26 shorter events, 0.9 us)
Async XLA Ops:
  0.6 25.4 %copy-start = (f32[16,128]{1,0:T(8,128)S(1)}, f32[16,128]{1,0:T(8,128)}, u32[]{:S(2)}) copy-start(f32[16,128]{1,0:T(8,128)} %param.18) | copy-start | bytes 24580
  0.6 2.7 %copy-start.4 = (s32[8,1]{0,1:T(1,128)S(1)}, s32[8,1]{0,1:T(1,128)}, u32[]{:S(2)}) copy-start(s32[8,1]{0,1:T(1,128)} %param.17) | copy-start | bytes 100
  0.7 2.8 %copy-start.2 = (f32[8,3,32,32]{3,2,1,0:T(8,128)S(1)}, f32[8,3,32,32]{3,2,1,0:T(8,128)}, u32[]{:S(2)}) copy-start(f32[8,3,32,32]{3,2,1,0:T(8,128)} %param.13) | copy-start | bytes 294916
  0.7 3.5 %copy-start.3 = (f32[8,3,32,32]{3,2,1,0:T(8,128)S(1)}, f32[8,3,32,32]{3,2,1,0:T(8,128)}, u32[]{:S(2)}) copy-start(f32[8,3,32,32]{3,2,1,0:T(8,128)} %param.14) | copy-start | bytes 294916
  1.5 3.5 %collective-permute-start = (s32[8,16]{1,0:T(8,128)S(1)}, s32[8,16]{1,0:T(8,128)S(1)}, u32[]{:S(2)}, u32[]{:S(2)}) collective-permute-start(s32[8,16]{1,0:T(8,128)S(1)} %fusion.6), channel_id=1, source_target_pairs={{0,1},{1,0},{2,3},{3,2},{4,5},{5,4},{6,7},{7,6},{8,9},{9,8},{10,11... | collective-permute-start | bytes 1544 | tf_op jit(solution)/shard_map/ppermute | solution.py:339
  3.2 2.8 %collective-permute-start.1 = (f32[4,16,32,32]{3,2,1,0:T(8,128)S(1)}, f32[4,16,32,32]{3,2,1,0:T(8,128)S(1)}, u32[]{:S(2)}, u32[]{:S(2)}) collective-permute-start(f32[4,16,32,32]{3,2,1,0:T(8,128)S(1)} %dynamic-slice_bitcast_fusion), channel_id=1, source_target_pairs={{0,1},{1,0},{2,3},{3,2},{4,5},{5,4},{6,7},{7,6},{8,9},{9,8},{10,11... | collective-permute-start | bytes 786440 | tf_op jit(solution)/shard_map/ppermute | solution.py:476
  6.0 1.0 copy-start.1
  19.7 22.5 %all-to-all-start.2 = ((f32[16,4,2,2,8,128]{5,4,3,2,1,0:T(8,128)}), f32[16,4,2,2,8,128]{5,4,3,2,1,0:T(8,128)S(1)}, u32[]{:S(2)}, u32[]{:S(2)}) async-start(f32[16,4,2,2,8,128]{5,4,3,2,1,0:T(8,128)} %get-tuple-element.16), calls=%async_computation.2 | async-start | bytes 2097152 | tf_op jit(solution)/shard_map/all_to_all | solution.py:505
  42.1 25.4 %all-to-all-start = ((f32[16,4,2,2,8,128]{5,4,3,2,1,0:T(8,128)}), f32[16,4,2,2,8,128]{5,4,3,2,1,0:T(8,128)S(1)}, u32[]{:S(2)}, u32[]{:S(2)}) async-start(f32[16,4,2,2,8,128]{5,4,3,2,1,0:T(8,128)} %get-tuple-element.13), calls=%async_computation | async-start | bytes 2097152 | tf_op jit(solution)/shard_map/all_to_all | solution.py:505
  46.5 17.1 %collective-permute-start.3 = (f32[16,4096]{1,0:T(8,128)S(1)}, f32[16,4096]{1,0:T(8,128)S(1)}, u32[]{:S(2)}, u32[]{:S(2)}) collective-permute-start(f32[16,4096]{1,0:T(8,128)S(1)} %partial_coefs.3.mine_ref), channel_id=1, source_target_pairs={{0,16},{16,0},{1,17},{17,1},{2,18},{18,2},{3,19},{19,3},{4,20},{20... | collective-permute-start | bytes 786440 | tf_op jit(solution)/shard_map/ppermute | solution.py:508
  67.5 25.0 %all-to-all-start.3 = ((f32[8,8,2,16,128]{4,3,2,1,0:T(8,128)}), f32[8,8,2,16,128]{4,3,2,1,0:T(8,128)S(1)}, u32[]{:S(2)}, u32[]{:S(2)}) async-start(f32[8,8,2,16,128]{4,3,2,1,0:T(8,128)} %bitcast.15), calls=%async_computation.3 | async-start | bytes 2097152 | tf_op jit(solution)/shard_map/all_to_all | solution.py:511
  73.9 16.0 %collective-permute-start.2 = (f32[16,4096]{1,0:T(8,128)S(1)}, f32[16,4096]{1,0:T(8,128)S(1)}, u32[]{:S(2)}, u32[]{:S(2)}) collective-permute-start(f32[16,4096]{1,0:T(8,128)S(1)} %partial_coefs.2.mine_ref), channel_id=1, source_target_pairs={{0,16},{16,0},{1,17},{17,1},{2,18},{18,2},{3,19},{19,3},{4,20},{20... | collective-permute-start | bytes 786440 | tf_op jit(solution)/shard_map/ppermute | solution.py:508
  92.5 18.0 %all-to-all-start.1 = ((f32[8,8,2,16,128]{4,3,2,1,0:T(8,128)}), f32[8,8,2,16,128]{4,3,2,1,0:T(8,128)S(1)}, u32[]{:S(2)}, u32[]{:S(2)}) async-start(f32[8,8,2,16,128]{4,3,2,1,0:T(8,128)} %bitcast.13), calls=%async_computation.1 | async-start | bytes 2097152 | tf_op jit(solution)/shard_map/all_to_all | solution.py:511

commit v6 on v5

--- a/solution.py
+++ b/solution.py
@@ -15,7 +15,7 @@
 LANES = 128
 SUBS = 8
 SMALL = 12 << 20
-LARGE = 60 << 20
+LARGE = 52 << 20
 
 
 def split_bf16(x):
@@ -76,10 +76,10 @@
 
 def step_kernel(
     n_e, spots, used, modes, width,
-    first_ref, table_ref,
+    table_ref,
     o_re, o_im, pr_hbm, pi_hbm, own_rec, par_rec, wf_hbm, wb_hbm, tw_hbm,
     out_re, out_im,
-    obj, rec, pr_ref, pi_ref, wf_ref, wb_ref, tw_ref, patch, term, root, work, sum_re, sum_im, sum_light, stage,
+    obj, rec, beam, probe, wf_ref, wb_ref, tw_ref, patch, term, root, work, sum_re, sum_im, sum_light, stage,
     obj_sem, rec_sem, shared_sem, out_sem,
 ):
     fold = LANES // width
@@ -87,7 +87,7 @@
     per_group = modes * SUBS
     per_q = groups * per_group
     side = obj.shape[3]
-    first = first_ref[0]
+    first = table_ref[0] >> (2 * side.bit_length() - 2 + spots.bit_length())
     dests = out_re.shape[0]
     sums = (sum_re, sum_im, sum_light)
 
@@ -113,8 +113,8 @@
         pltpu.make_async_copy(src, dst, shared_sem.at[n])
         for n, (src, dst) in enumerate(
             (
-                (pr_hbm.at[pl.ds(first, n_e)], pr_ref),
-                (pi_hbm.at[pl.ds(first, n_e)], pi_ref),
+                (pr_hbm.at[pl.ds(first, n_e)], beam.at[0]),
+                (pi_hbm.at[pl.ds(first, n_e)], beam.at[1]),
                 (tw_hbm, tw_ref),
                 (wf_hbm, wf_ref),
                 (wb_hbm, wb_ref),
@@ -123,18 +123,15 @@
     ]
     for c in in_copies(0) + shared:
         c.start()
-    for e in range(1, n_e):
-        for c in in_copies(e):
-            c.start()
     lane = lax.broadcasted_iota(jnp.int32, (SUBS, LANES), 1)
     block = lane // width
     for c in shared:
         c.wait()
 
     def place(e, index):
-        packed = table_ref[(first + e) * used + index]
+        packed = table_ref[e * used + index]
         shift = side.bit_length() - 1
-        return packed >> (2 * shift), (packed >> shift) & (side - 1), packed & (side - 1)
+        return (packed >> (2 * shift)) & (2 * spots - 1), (packed >> shift) & (side - 1), packed & (side - 1)
 
     def merge(parts):
         out = parts[0]
@@ -155,6 +152,17 @@
             acc[...] = jnp.zeros_like(acc)
         for c in in_copies(e):
             c.wait()
+
+        @pl.when(e + 1 < n_e)
+        def _():
+            for c in in_copies(e + 1):
+                c.start()
+
+        for c in range(2):
+            for m in range(modes):
+                probe[c, m] = jnp.concatenate(
+                    [beam[c, e, m, pl.ds(i, SUBS, stride=fold), :] for i in range(fold)], axis=1
+                )
         for s in range(used):
             slot, row, col = place(e, s)
             low = lane >= col
@@ -177,8 +185,8 @@
             for m in range(modes):
                 x_re, x_im = [], []
                 for t in range(SUBS):
-                    p_re = row_of(pr_ref, e, m, pl.ds(t, 1), slice(None))
-                    p_im = row_of(pi_ref, e, m, pl.ds(t, 1), slice(None))
+                    p_re = row_of(probe, 0, m, pl.ds(t, 1), slice(None))
+                    p_im = row_of(probe, 1, m, pl.ds(t, 1), slice(None))
                     x_re.append(p_re * w_re[t] - p_im * w_im[t])
                     x_im.append(p_re * w_im[t] + p_im * w_re[t])
                 y_re, y_im = fft8(x_re, x_im, -1)
@@ -215,7 +223,7 @@
 
         light = jnp.zeros((SUBS, LANES), jnp.float32)
         for m in range(modes):
-            a, b = pr_ref[e, m], pi_ref[e, m]
+            a, b = probe[0, m], probe[1, m]
             light = light + a * a + b * b
 
         for g in range(groups):
@@ -234,8 +242,8 @@
                     x_im.append(b)
                 y_re, y_im = fft8(x_re, x_im, 1)
                 for t in range(SUBS):
-                    p_re = row_of(pr_ref, e, m, pl.ds(t, 1), slice(None))
-                    p_im = row_of(pi_ref, e, m, pl.ds(t, 1), slice(None))
+                    p_re = row_of(probe, 0, m, pl.ds(t, 1), slice(None))
+                    p_im = row_of(probe, 1, m, pl.ds(t, 1), slice(None))
                     a = p_re * y_re[t] + p_im * y_im[t]
                     b = p_re * y_im[t] - p_im * y_re[t]
                     t_re[t] = a if m == 0 else t_re[t] + a
@@ -267,7 +275,7 @@
             for u in range(SUBS):
                 n = k * SUBS + u
                 at = pl.ds(pl.multiple_of(n * SUBS, SUBS), SUBS)
-                dest, far = n % dests, n // dests
+                dest, far = n & (dests - 1), n >> (dests.bit_length() - 1)
                 mid = [pltpu.roll(acc[2, at, :], LANES // 2, 1) for acc in sums]
                 for h in range(2):
                     mine = high if h == 0 else ~high
@@ -288,7 +296,7 @@
             c.wait()
 
 
-def gradient_step(objects, beams, own_rec, par_rec, table, first, n_e, used, fars):
+def gradient_step(objects, beams, own_rec, par_rec, table, n_e, used, fars):
     o_re, o_im = objects
     local, side, _ = o_re.shape
     modes, width = beams[0].shape[1], beams[0].shape[-1]
@@ -296,21 +304,21 @@
     flat = width * width // LANES
     assert flat == SUBS and side == 2 * LANES and used % SUBS == 0
     wf, wb, tw = transform_tables(width)
-    shaped = [b.reshape(local, modes, flat, LANES) for b in beams]
     hbm = pl.BlockSpec(memory_space=pl.ANY)
     out_shape = (side // SUBS // fars, n_e, fars, side // LANES, SUBS, LANES)
     return pl.pallas_call(
         functools.partial(step_kernel, n_e, spots, used, modes, width),
         out_shape=[jax.ShapeDtypeStruct(out_shape, jnp.float32)] * 2,
         grid_spec=pltpu.PrefetchScalarGridSpec(
-            num_scalar_prefetch=2,
+            num_scalar_prefetch=1,
             grid=(1,),
             in_specs=[hbm] * 9,
             out_specs=[hbm, hbm],
             scratch_shapes=[
                 pltpu.VMEM((n_e, 2, 2, side, LANES), jnp.float32),
                 pltpu.VMEM((n_e, 2 * spots, width, width), jnp.float32),
-                *[pltpu.VMEM((n_e, modes, flat, LANES), jnp.float32)] * 2,
+                pltpu.VMEM((2, n_e, modes, width, width), jnp.float32),
+                pltpu.VMEM((2, modes, flat, LANES), jnp.float32),
                 *[pltpu.VMEM(wf.shape, jnp.bfloat16)] * 2,
                 pltpu.VMEM(tw.shape, jnp.float32),
                 pltpu.VMEM((2, used * SUBS, LANES), jnp.float32),
@@ -328,16 +336,20 @@
         compiler_params=pltpu.CompilerParams(vmem_limit_bytes=LARGE),
         name="gradient_step",
     )(
-        first, table, o_re, o_im, *shaped, own_rec, par_rec,
+        table, o_re, o_im, *beams, own_rec, par_rec,
         jnp.asarray(wf), jnp.asarray(wb), jnp.asarray(tw),
     )
 
 
-def slot_table(corners, counts, side, used, swap):
-    local, spots, _ = corners.shape
-    packed = corners[..., 0] * side + corners[..., 1]
-    both = jnp.concatenate([packed, lax.ppermute(packed, "ta", swap)], axis=1)
-    both = both + jnp.arange(2 * spots, dtype=jnp.int32) * (side * side)
+def slot_table(corners, theirs, counts, first, n_e, side):
+    spots = corners.shape[1]
+    used = spots * 3 // 2
+    assert side & (side - 1) == 0 and spots & (spots - 1) == 0
+    both = jnp.concatenate([corners, theirs], axis=1)
+    both = lax.dynamic_slice_in_dim(both, first, n_e, 0)
+    counts = lax.dynamic_slice_in_dim(counts, first, n_e, 0)
+    both = both[..., 0] * side + both[..., 1]
+    both = both + (first * 2 * spots + jnp.arange(2 * spots, dtype=jnp.int32)) * (side * side)
     index = jnp.arange(used, dtype=jnp.int32)[None]
     index = index + jnp.where(index < counts, 0, spots - counts)
     chosen = index[:, :, None] == jnp.arange(2 * spots, dtype=jnp.int32)
@@ -472,16 +484,18 @@
     two_level = divided and pix == SUBS * side and local_energies == SUBS
     own_rec = recorded_diffraction[:, 0]
     first = tile * n_e if divided else jnp.zeros((), jnp.int32)
+    theirs = lax.ppermute(window_corners, "ta", swap)
     give = lax.dynamic_slice_in_dim(own_rec, (1 - tile) * n_e, n_e, 0) if divided else own_rec
     par_rec = lax.ppermute(give, "ta", swap)
-    table = slot_table(window_corners[:, 0], filled_tallies, side, used, swap)
+    table = slot_table(
+        window_corners[:, 0], theirs[:, 0], filled_tallies, first.astype(jnp.int32), n_e, side
+    )
     stepped = gradient_step(
         (sample_inphase, sample_quadrature),
         (beam_inphase, beam_quadrature),
         own_rec,
         par_rec,
         table,
-        first.astype(jnp.int32)[None],
         n_e,
         used,
         fars if two_level else 1,

time: 112 us -> 109 us (0.973)
  local copies, waits for them, and re-layouts: 5.61 us -> 1.74 us
  waiting for transfers between devices: 56.7 us -> 58.8 us
  Pallas kernels: 19.6 us -> 18.4 us
    ppermute x1, waiting for transfers between devices: 0.01 us -> 2.09 us  [local(): par_rec = lax.ppermute(give, 'ta', swap)]
    unnamed x12 -> x17, local copies, waits for them, and re-layouts: 1.85 us -> 0.13 us
    reshape x2 -> x0, local copies, waits for them, and re-layouts: 1.57 us -> none  [gradient_step(): shaped = [b.reshape(local, modes, flat, LANES) for b in beams]]
    pallas_call x1, Pallas kernels: 12.6 us -> 11.4 us  [gradient_step(): pl.pallas_call(functools.partial(step_kernel, n_e, spots, used, modes, wi...]
  transfers between devices with their start and end apart: 8 -> 8, of which waited for: 6 -> 7; matrix products, arithmetic and copies ran while one was open for 9% -> 7% of each run, Pallas kernels for 5% -> 6%
where the time goes in v6:
time: 109 us; the launch traced here: 108 us
  waiting for transfers between devices  58.8 us (54%)
  starting transfers between devices  23 us (21%)
  Pallas kernels  18.4 us (17%)
  other arithmetic  5.22 us (5%)
  local copies, waits for them, and re-layouts  1.74 us (2%)
    ppermute x2, waiting for transfers between devices, local(): theirs = lax.ppermute(mine, 'far', swap)  30.5 us
    all_to_all x2, waiting for transfers between devices, local(): lax.all_to_all(x, ('cube', 'ta'), 0, 0, tiled=True)  13.5 us
    all_to_all x2, waiting for transfers between devices, local(): lax.all_to_all(fit.reshape(cube, local_energies, fars, pix // LANES, LANE...  12.7 us
    pallas_call x1, Pallas kernels, gradient_step(): pl.pallas_call(functools.partial(step_kernel, n_e, spots, used, modes, wi...  11.4 us
    all_to_all x2, starting transfers between devices, local(): lax.all_to_all(fit.reshape(cube, local_energies, fars, pix // LANES, LANE...  10 us
    all_to_all x2, starting transfers between devices, local(): lax.all_to_all(x, ('cube', 'ta'), 0, 0, tiled=True)  9.63 us
    pallas_call x2, Pallas kernels, fitted_values(): pl.pallas_call(fit_kernel, out_shape=[jax.ShapeDtypeStruct((edges, own),...  3.59 us
    ppermute x2, starting transfers between devices, local(): theirs = lax.ppermute(mine, 'far', swap)  2.62 us
  transfers between devices with their start and end apart: 8, of which 7 were waited for; matrix products, arithmetic and copies ran while one was open for 7% of the time, Pallas kernels for 6%

profile of v6, /device:TPU:0, one launch (start us, length us, event | category | flops | bytes accessed | tf_op | source)
XLA Modules:
  0.0 108.4 jit_solution(10315671884292013933)
XLA Ops:
  0.7 0.6 collective-permute-start
  1.3 1.3 %dynamic-slice_bitcast_fusion = f32[4,16,32,32]{3,2,1,0:T(8,128)S(1)} fusion(f32[8,1,16,32,32]{4,3,2,1,0:T(8,128)} %param.15, s32[]{:T(128)S(6)} %select_n.30), kind=kLoop, calls=%fused_computation | loop fusion | bytes 524292 | tf_op jit(solution)/shard_map/dynamic_slice | solution.py:488
  2.6 0.2 collective-permute-start.1
  3.0 0.2 select_reduce_fusion
  3.3 2.1 %collective-permute-done.1.par_rec = f32[4,16,32,32]{3,2,1,0:T(8,128)} collective-permute-done((f32[4,16,32,32]{3,2,1,0:T(8,128)S(1)}, f32[4,16,32,32]{3,2,1,0:T(8,128)}, u32[]{:S(2)}, u32[]{:S(2)}) %collective-permute-start.1) | collective-permute-done | bytes 262176 | tf_op jit(solution)/shard_map/ppermute | solution.py:489
  5.5 11.4 %gradient_step.1 = (f32[16,4,2,2,8,128]{5,4,3,2,1,0:T(8,128)}, f32[16,4,2,2,8,128]{5,4,3,2,1,0:T(8,128)}) custom-call(s32[96]{0:T(128)S(1)} %reshape.111.table_ref, f32[8,256,256]{2,1,0:T(8,128)} %o_re.1, f32[8,256,256]{2,1,0:T(8,128)} %o_im.1, f32[8,3,32,32]{3,2,1,0:T(8,128)S(1)} %copy-done.1, f32[8,3,32,32]{3,2,1,0:T(8,128)S(1)} %copy-done.2, ...), custom_call_target="tpu_custom_call" | custom-call | tf_op jit(solution)/shard_map/gradient_step/pallas_call | solution.py:309
  16.8 6.0 %all-to-all-start.2 = ((f32[16,4,2,2,8,128]{5,4,3,2,1,0:T(8,128)}), f32[16,4,2,2,8,128]{5,4,3,2,1,0:T(8,128)S(1)}, u32[]{:S(2)}, u32[]{:S(2)}) async-start(f32[16,4,2,2,8,128]{5,4,3,2,1,0:T(8,128)} %get-tuple-element.16), calls=%async_computation.2 | async-start | bytes 2097152 | tf_op jit(solution)/shard_map/all_to_all | solution.py:519
  22.8 0.1 fusion.8
  23.0 1.5 %cholesky.16 = f32[16,16]{1,0:T(8,128)S(1)} custom-call(f32[16,16]{1,0:T(8,128)S(1)} %fusion.5), custom_call_target="Cholesky" | custom-call | tf_op jit(solution)/shard_map/jit(cholesky)/cholesky | solution.py:504
  24.5 0.7 compare_reduce_fusion
  25.2 0.6 fusion
  25.9 1.2 %custom-call.10 = f32[1,16,16]{1,2,0:T(8,128)S(1)} custom-call(f32[1,16,16]{2,1,0:T(8,128)S(1)} %fusion), custom_call_target="InvertDiagBlocksLowerTriangular" | custom-call | tf_op jit(solution)/shard_map/jit(_cho_solve)/triangular_solve | solution.py:505
  27.2 0.1 copy.20
  27.3 0.2 fusion.3
  27.5 0.1 fusion.1
  27.7 11.3 %all-to-all-done.2 = f32[16,4,2,2,8,128]{5,4,3,2,1,0:T(8,128)S(1)} async-done(((f32[16,4,2,2,8,128]{5,4,3,2,1,0:T(8,128)}), f32[16,4,2,2,8,128]{5,4,3,2,1,0:T(8,128)S(1)}, u32[]{:S(2)}, u32[]{:S(2)}) %all-to-all-start.2) | async-done | bytes 1048608 | tf_op jit(solution)/shard_map/all_to_all | solution.py:519
  39.0 3.7 %all-to-all-start = ((f32[16,4,2,2,8,128]{5,4,3,2,1,0:T(8,128)}), f32[16,4,2,2,8,128]{5,4,3,2,1,0:T(8,128)S(1)}, u32[]{:S(2)}, u32[]{:S(2)}) async-start(f32[16,4,2,2,8,128]{5,4,3,2,1,0:T(8,128)} %get-tuple-element.13), calls=%async_computation | async-start | bytes 2097152 | tf_op jit(solution)/shard_map/all_to_all | solution.py:519
  42.6 0.7 partial_coefs.3.mine_ref
  43.3 2.6 %collective-permute-start.3 = (f32[16,4096]{1,0:T(8,128)S(1)}, f32[16,4096]{1,0:T(8,128)S(1)}, u32[]{:S(2)}, u32[]{:S(2)}) collective-permute-start(f32[16,4096]{1,0:T(8,128)S(1)} %partial_coefs.3.mine_ref), channel_id=1, source_target_pairs={{0,16},{16,0},{1,17},{17,1},{2,18},{18,2},{3,19},{19,3},{4,20},{20... | collective-permute-start | bytes 786440 | tf_op jit(solution)/shard_map/ppermute | solution.py:522
  45.9 14.4 %collective-permute-done.3.theirs_ref = f32[16,4096]{1,0:T(8,128)S(1)} collective-permute-done((f32[16,4096]{1,0:T(8,128)S(1)}, f32[16,4096]{1,0:T(8,128)S(1)}, u32[]{:S(2)}, u32[]{:S(2)}) %collective-permute-start.3) | collective-permute-done | bytes 262176 | tf_op jit(solution)/shard_map/ppermute | solution.py:522
  60.4 1.8 %fitted_values.3 = (f32[16,2048]{1,0:T(8,128)S(1)}, f32[2048,128]{1,0:T(8,128)}) custom-call(s32[1]{0:T(128)} %bitcast.far_ref, f32[16,4096]{1,0:T(8,128)S(1)} %partial_coefs.3.mine_ref, f32[16,4096]{1,0:T(8,128)S(1)} %collective-permute-done.3.theirs_ref, f32[64,16]{1,0:T(8,128)S(1)} %bitcast.36), custom_call_target="tpu_custom_call" | custom-call | flops 25165824 | bytes 1048576 | tf_op jit(solution)/shard_map/fitted_values/pallas_call | solution.py:416
  62.2 2.2 %all-to-all-done = f32[16,4,2,2,8,128]{5,4,3,2,1,0:T(8,128)S(1)} async-done(((f32[16,4,2,2,8,128]{5,4,3,2,1,0:T(8,128)}), f32[16,4,2,2,8,128]{5,4,3,2,1,0:T(8,128)S(1)}, u32[]{:S(2)}, u32[]{:S(2)}) %all-to-all-start) | async-done | bytes 1048608 | tf_op jit(solution)/shard_map/all_to_all | solution.py:519
  64.3 5.7 %all-to-all-start.3 = ((f32[8,8,2,16,128]{4,3,2,1,0:T(8,128)}), f32[8,8,2,16,128]{4,3,2,1,0:T(8,128)S(1)}, u32[]{:S(2)}, u32[]{:S(2)}) async-start(f32[8,8,2,16,128]{4,3,2,1,0:T(8,128)} %bitcast.15), calls=%async_computation.3 | async-start | bytes 2097152 | tf_op jit(solution)/shard_map/all_to_all | solution.py:525
  70.0 0.7 partial_coefs.2.mine_ref
  70.7 16.0 %collective-permute-done.2.theirs_ref = f32[16,4096]{1,0:T(8,128)S(1)} collective-permute-done((f32[16,4096]{1,0:T(8,128)S(1)}, f32[16,4096]{1,0:T(8,128)S(1)}, u32[]{:S(2)}, u32[]{:S(2)}) %collective-permute-start.2) | collective-permute-done | bytes 262176 | tf_op jit(solution)/shard_map/ppermute | solution.py:522
  86.7 1.8 %fitted_values.2 = (f32[16,2048]{1,0:T(8,128)S(1)}, f32[2048,128]{1,0:T(8,128)}) custom-call(s32[1]{0:T(128)} %bitcast.far_ref, f32[16,4096]{1,0:T(8,128)S(1)} %partial_coefs.2.mine_ref, f32[16,4096]{1,0:T(8,128)S(1)} %collective-permute-done.2.theirs_ref, f32[64,16]{1,0:T(8,128)S(1)} %bitcast.37), custom_call_target="tpu_custom_call" | custom-call | flops 25165824 | bytes 1048576 | tf_op jit(solution)/shard_map/fitted_values/pallas_call | solution.py:416
  88.5 0.8 all-to-all-done.3.in_ref
  89.4 4.3 %all-to-all-start.1 = ((f32[8,8,2,16,128]{4,3,2,1,0:T(8,128)}), f32[8,8,2,16,128]{4,3,2,1,0:T(8,128)S(1)}, u32[]{:S(2)}, u32[]{:S(2)}) async-start(f32[8,8,2,16,128]{4,3,2,1,0:T(8,128)} %bitcast.13), calls=%async_computation.1 | async-start | bytes 2097152 | tf_op jit(solution)/shard_map/all_to_all | solution.py:525
  93.7 0.7 pad_maximum_fusion
  94.4 1.0 gather_part.2.refs_0_
  95.5 11.9 %all-to-all-done.1.in_ref = f32[8,8,2,16,128]{4,3,2,1,0:T(8,128)S(1)} async-done(((f32[8,8,2,16,128]{4,3,2,1,0:T(8,128)}), f32[8,8,2,16,128]{4,3,2,1,0:T(8,128)S(1)}, u32[]{:S(2)}, u32[]{:S(2)}) %all-to-all-start.1) | async-done | bytes 1048608 | tf_op jit(solution)/shard_map/all_to_all | solution.py:525
  107.4 1.0 gather_part.3
  (30 shorter events, 0.7 us)
Async XLA Ops:
  0.6 22.2 %copy-start = (f32[16,128]{1,0:T(8,128)S(1)}, f32[16,128]{1,0:T(8,128)}, u32[]{:S(2)}) copy-start(f32[16,128]{1,0:T(8,128)} %param.18) | copy-start | bytes 24580
  0.6 4.8 %copy-start.5 = (f32[16,128]{1,0:T(8,128)S(1)}, f32[16,128]{1,0:T(8,128)}, u32[]{:S(2)}) copy-start(f32[16,128]{1,0:T(8,128)} %constant.88.clone.tw_hbm) | copy-start | bytes 24580
  0.7 4.8 %copy-start.3 = (bf16[768,256]{1,0:T(8,128)(2,1)S(1)}, bf16[768,256]{1,0:T(8,128)(2,1)}, u32[]{:S(2)}) copy-start(bf16[768,256]{1,0:T(8,128)(2,1)} %constant.87.clone.wb_hbm) | copy-start | bytes 1179652
  0.7 4.8 %copy-start.4 = (bf16[768,256]{1,0:T(8,128)(2,1)S(1)}, bf16[768,256]{1,0:T(8,128)(2,1)}, u32[]{:S(2)}) copy-start(bf16[768,256]{1,0:T(8,128)(2,1)} %constant.86.clone.wf_hbm) | copy-start | bytes 1179652
  0.7 2.3 %copy-start.6 = (s32[8,1,16,2]{2,3,1,0:T(2,128)S(1)}, s32[8,1,16,2]{2,3,1,0:T(2,128)}, u32[]{:S(2)}) copy-start(s32[8,1,16,2]{2,3,1,0:T(2,128)} %param.16) | copy-start | bytes 3076
  0.7 2.1 %copy-start.7 = (s32[8,1]{0,1:T(1,128)S(1)}, s32[8,1]{0,1:T(1,128)}, u32[]{:S(2)}) copy-start(s32[8,1]{0,1:T(1,128)} %param.17) | copy-start | bytes 100
  0.7 4.7 %copy-start.2 = (f32[8,3,32,32]{3,2,1,0:T(8,128)S(1)}, f32[8,3,32,32]{3,2,1,0:T(8,128)}, u32[]{:S(2)}) copy-start(f32[8,3,32,32]{3,2,1,0:T(8,128)} %pi_hbm.1) | copy-start | bytes 294916
  0.7 4.7 %copy-start.1 = (f32[8,3,32,32]{3,2,1,0:T(8,128)S(1)}, f32[8,3,32,32]{3,2,1,0:T(8,128)}, u32[]{:S(2)}) copy-start(f32[8,3,32,32]{3,2,1,0:T(8,128)} %pr_hbm.1) | copy-start | bytes 294916
  0.7 2.2 %collective-permute-start = (s32[8,1,16,2]{2,3,1,0:T(2,128)}, s32[8,1,16,2]{2,3,1,0:T(2,128)S(1)}, u32[]{:S(2)}, u32[]{:S(2)}) collective-permute-start(s32[8,1,16,2]{2,3,1,0:T(2,128)} %param.16), channel_id=1, source_target_pairs={{0,1},{1,0},{2,3},{3,2},{4,5},{5,4},{6,7},{7,6},{8,9},{9,8},{10,11... | collective-permute-start | bytes 3080 | tf_op jit(solution)/shard_map/ppermute | solution.py:487
  2.6 2.9 %collective-permute-start.1 = (f32[4,16,32,32]{3,2,1,0:T(8,128)S(1)}, f32[4,16,32,32]{3,2,1,0:T(8,128)}, u32[]{:S(2)}, u32[]{:S(2)}) collective-permute-start(f32[4,16,32,32]{3,2,1,0:T(8,128)S(1)} %dynamic-slice_bitcast_fusion), channel_id=1, source_target_pairs={{0,1},{1,0},{2,3},{3,2},{4,5},{5,4},{6,7},{7,6},{8,9},{9,8},{10,11... | collective-permute-start | bytes 786440 | tf_op jit(solution)/shard_map/ppermute | solution.py:489
  16.8 22.1 %all-to-all-start.2 = ((f32[16,4,2,2,8,128]{5,4,3,2,1,0:T(8,128)}), f32[16,4,2,2,8,128]{5,4,3,2,1,0:T(8,128)S(1)}, u32[]{:S(2)}, u32[]{:S(2)}) async-start(f32[16,4,2,2,8,128]{5,4,3,2,1,0:T(8,128)} %get-tuple-element.16), calls=%async_computation.2 | async-start | bytes 2097152 | tf_op jit(solution)/shard_map/all_to_all | solution.py:519
  39.0 25.4 %all-to-all-start = ((f32[16,4,2,2,8,128]{5,4,3,2,1,0:T(8,128)}), f32[16,4,2,2,8,128]{5,4,3,2,1,0:T(8,128)S(1)}, u32[]{:S(2)}, u32[]{:S(2)}) async-start(f32[16,4,2,2,8,128]{5,4,3,2,1,0:T(8,128)} %get-tuple-element.13), calls=%async_computation | async-start | bytes 2097152 | tf_op jit(solution)/shard_map/all_to_all | solution.py:519
  43.3 17.1 %collective-permute-start.3 = (f32[16,4096]{1,0:T(8,128)S(1)}, f32[16,4096]{1,0:T(8,128)S(1)}, u32[]{:S(2)}, u32[]{:S(2)}) collective-permute-start(f32[16,4096]{1,0:T(8,128)S(1)} %partial_coefs.3.mine_ref), channel_id=1, source_target_pairs={{0,16},{16,0},{1,17},{17,1},{2,18},{18,2},{3,19},{19,3},{4,20},{20... | collective-permute-start | bytes 786440 | tf_op jit(solution)/shard_map/ppermute | solution.py:522
  64.3 25.0 %all-to-all-start.3 = ((f32[8,8,2,16,128]{4,3,2,1,0:T(8,128)}), f32[8,8,2,16,128]{4,3,2,1,0:T(8,128)S(1)}, u32[]{:S(2)}, u32[]{:S(2)}) async-start(f32[8,8,2,16,128]{4,3,2,1,0:T(8,128)} %bitcast.15), calls=%async_computation.3 | async-start | bytes 2097152 | tf_op jit(solution)/shard_map/all_to_all | solution.py:525
  70.7 16.0 %collective-permute-start.2 = (f32[16,4096]{1,0:T(8,128)S(1)}, f32[16,4096]{1,0:T(8,128)S(1)}, u32[]{:S(2)}, u32[]{:S(2)}) collective-permute-start(f32[16,4096]{1,0:T(8,128)S(1)} %partial_coefs.2.mine_ref), channel_id=1, source_target_pairs={{0,16},{16,0},{1,17},{17,1},{2,18},{18,2},{3,19},{19,3},{4,20},{20... | collective-permute-start | bytes 786440 | tf_op jit(solution)/shard_map/ppermute | solution.py:522
  89.4 18.0 %all-to-all-start.1 = ((f32[8,8,2,16,128]{4,3,2,1,0:T(8,128)}), f32[8,8,2,16,128]{4,3,2,1,0:T(8,128)S(1)}, u32[]{:S(2)}, u32[]{:S(2)}) async-start(f32[8,8,2,16,128]{4,3,2,1,0:T(8,128)} %bitcast.13), calls=%async_computation.1 | async-start | bytes 2097152 | tf_op jit(solution)/shard_map/all_to_all | solution.py:525
